TPU v7x, 256 devices: a whole 4x4x8 slice. The times are simulated.
256 devices in a mesh: outer: 16 (over y_hi, x, core), inner: 16 (over y_lo, z).
Axes of the slice: x: 4, y: 4 (y_hi: 2, y_lo: 2; y = y_hi * 2 + y_lo), z: 8, core: 2. Of those that a mesh axis runs over, the one named last changes fastest.
Arguments:
- projected: bfloat16 [32768, 12288], P(('outer', 'inner')), may hold values from -6 to 6
- short_taps: float32 [3, 12288], replicated, may hold values from -3 to 3
- rates: float32 [4096, 16], replicated, may hold values from 7.6293945e-06 to 0.05
- residues: float32 [4096, 16], replicated, may hold values from -1.5 to 1.5
- skip_gain: float32 [4096], replicated, may hold values from -4 to 4
Outputs:
- gated: bfloat16 [32768, 4096], P(('outer', 'inner'))
All inputs are finite; a program needn't handle non-finite values.
Results may differ from a plain program's by a relative error of at most 0.008.
Values may be sent and summed in bfloat16 or wider, within the bound.
A program may use at most 128 MiB of HBM per device.

v0:
```python
import jax
import jax.numpy as jnp
from jax import lax
from jax.sharding import PartitionSpec as P

TWO_PI = 2.0 * 3.141592653589793


def passed_along(value, axis, steps):
    count = lax.axis_size(axis)
    leading, last = (max(0, -steps), min(count, count - steps))
    return lax.ppermute(value, axis, [(source, source + steps) for source in range(leading, last)])


def in_blocks(array, dim, peers):
    lengths = array.shape
    blocks = array.reshape(*lengths[:dim], peers, lengths[dim] // peers, *lengths[dim + 1 :])
    return jnp.moveaxis(blocks, dim, 0)


def joined_along(blocks, dim):
    blocks = jnp.moveaxis(blocks, 0, dim)
    lengths = blocks.shape
    return blocks.reshape(*lengths[:dim], lengths[dim] * lengths[dim + 1], *lengths[dim + 2 :])


def exchange_both(array, axis, axes, splits, concats):
    sizes = [lax.axis_size(a) for a in axes]
    blocks = in_blocks(array, splits[0], sizes[0])
    blocks = jnp.moveaxis(in_blocks(blocks, splits[1] + 1, sizes[1]), 0, 1)
    inside = blocks.shape[2:]
    blocks = blocks.reshape(-1, *inside)
    blocks = lax.all_to_all(blocks, axis, split_axis=0, concat_axis=0, tiled=True)
    blocks = joined_along(blocks.reshape(*sizes, *inside), concats[0] + 1)
    return joined_along(blocks, concats[1])


def phase_table(count_rows, count_cols, modulus, sign):
    product = (
        jnp.arange(count_rows, dtype=jnp.int32)[:, None]
        * jnp.arange(count_cols, dtype=jnp.int32)[None, :]
        % modulus
    )
    angle = sign * TWO_PI / modulus * product.astype(jnp.float32)
    return (jnp.cos(angle), jnp.sin(angle))


def complex_times(left_re, left_im, right_re, right_im):
    return (left_re * right_re - left_im * right_im, left_re * right_im + left_im * right_re)


def middle_segment(
    sec_re, sec_im, k_values, ko_count, inner_count, rows, rates, residues, chan_start, chan_local
):
    full_blocks = ko_count * inner_count
    length = full_blocks * rows
    tokens_total = length // 2
    inner_re, inner_im = phase_table(inner_count, inner_count, inner_count, -1.0)
    mid_re = jnp.einsum("ji,ckis->ckjs", inner_re, sec_re) - jnp.einsum(
        "ji,ckis->ckjs", inner_im, sec_im
    )
    mid_im = jnp.einsum("ji,ckis->ckjs", inner_re, sec_im) + jnp.einsum(
        "ji,ckis->ckjs", inner_im, sec_re
    )
    block_freq = k_values[:, None] + ko_count * jnp.arange(inner_count, dtype=jnp.int32)[None, :]
    spots = jnp.arange(rows, dtype=jnp.int32)
    twist = (
        -TWO_PI
        / length
        * (block_freq[:, :, None] * spots[None, None, :] % length).astype(jnp.float32)
    )
    twist_re = jnp.cos(twist)[None]
    twist_im = jnp.sin(twist)[None]
    mid_re, mid_im = complex_times(mid_re, mid_im, twist_re, twist_im)
    local_re, local_im = phase_table(rows, rows, rows, -1.0)
    spec_re = jnp.einsum("ckjs,sq->ckjq", mid_re, local_re) - jnp.einsum(
        "ckjs,sq->ckjq", mid_im, local_im
    )
    spec_im = jnp.einsum("ckjs,sq->ckjq", mid_re, local_im) + jnp.einsum(
        "ckjs,sq->ckjq", mid_im, local_re
    )
    freq = block_freq[:, :, None] + full_blocks * jnp.arange(rows, dtype=jnp.int32)[None, None, :]
    angle = -TWO_PI / length * freq.astype(jnp.float32)
    half_sine = jnp.sin(0.5 * angle)[None]
    full_sine = jnp.sin(angle)[None]
    parity = (1 - 2 * (freq % 2)).astype(jnp.float32)[None]
    my_rates = lax.dynamic_slice_in_dim(rates, chan_start, chan_local, 0)
    my_residues = lax.dynamic_slice_in_dim(residues, chan_start, chan_local, 0)
    filter_re = jnp.zeros(spec_re.shape, jnp.float32)
    filter_im = jnp.zeros(spec_re.shape, jnp.float32)
    for mode in range(rates.shape[1]):
        rate = my_rates[:, mode][:, None, None, None]
        decay = jnp.exp(-rate)
        amplitude = my_residues[:, mode][:, None, None, None] * jnp.sqrt(2.0 * rate)
        numer = amplitude * (1.0 - jnp.exp(-rate * tokens_total) * parity)
        denom_re = -jnp.expm1(-rate) + 2.0 * decay * half_sine * half_sine
        denom_im = -decay * full_sine
        magnitude = denom_re * denom_re + denom_im * denom_im
        filter_re = filter_re + numer * denom_re / magnitude
        filter_im = filter_im - numer * denom_im / magnitude
    prod_re, prod_im = complex_times(spec_re, spec_im, filter_re, filter_im)
    back_re = jnp.einsum("ckjq,sq->ckjs", prod_re, local_re) + jnp.einsum(
        "ckjq,sq->ckjs", prod_im, local_im
    )
    back_im = jnp.einsum("ckjq,sq->ckjs", prod_im, local_re) - jnp.einsum(
        "ckjq,sq->ckjs", prod_re, local_im
    )
    back_re, back_im = complex_times(back_re, back_im, twist_re, -twist_im)
    undo_re = jnp.einsum("ji,ckjs->ckis", inner_re, back_re) + jnp.einsum(
        "ji,ckjs->ckis", inner_im, back_im
    )
    undo_im = jnp.einsum("ji,ckjs->ckis", inner_re, back_im) - jnp.einsum(
        "ji,ckjs->ckis", inner_im, back_re
    )
    return (undo_re, undo_im)


def on_device(projected, short_taps, rates, residues, skip_gain):
    rows = projected.shape[0]
    feature_width = projected.shape[1]
    channels = feature_width // 3
    outer_count = lax.axis_size("outer")
    inner_count = lax.axis_size("inner")
    outer_place = lax.axis_index("outer")
    inner_place = lax.axis_index("inner")
    previous = passed_along(projected[rows - 2 :], ("outer", "inner"), 1)
    padded = jnp.concatenate([previous, projected], 0).astype(jnp.float32)
    feat = short_taps[0] * padded[2:] + short_taps[1] * padded[1:-1] + short_taps[2] * padded[:-2]
    query = feat[:, :channels]
    mixed = feat[:, channels : 2 * channels] * feat[:, 2 * channels :]
    segmented = mixed.T
    ko_count = 2 * outer_count
    full_blocks = ko_count * inner_count
    length = full_blocks * rows
    chan_local = channels // (outer_count * inner_count)
    chan_start = (outer_place * inner_count + inner_place) * chan_local
    sections = segmented.reshape(outer_count, inner_count, chan_local, 1, 1, rows)
    gathered = exchange_both(
        sections.astype(jnp.bfloat16), ("outer", "inner"), ("outer", "inner"), (0, 1), (3, 4)
    ).astype(sections.dtype)
    signal = gathered.reshape(chan_local, outer_count, inner_count, rows)
    i_values = jnp.arange(inner_count, dtype=jnp.int32)
    outer_re, outer_im = phase_table(ko_count, outer_count, ko_count, -1.0)
    spin_re = jnp.einsum("ko,cois->ckis", outer_re, signal)
    spin_im = jnp.einsum("ko,cois->ckis", outer_im, signal)
    ko_axis = jnp.arange(ko_count, dtype=jnp.int32)
    turn = (
        -TWO_PI
        / full_blocks
        * (ko_axis[:, None] * i_values[None, :] % full_blocks).astype(jnp.float32)
    )
    first_re = jnp.cos(turn)[None, :, :, None]
    first_im = jnp.sin(turn)[None, :, :, None]
    spin_re, spin_im = complex_times(spin_re, spin_im, first_re, first_im)
    undo_re, undo_im = middle_segment(
        spin_re,
        spin_im,
        ko_axis,
        ko_count,
        inner_count,
        rows,
        rates,
        residues,
        chan_start,
        chan_local,
    )
    home_re, home_im = (undo_re, undo_im)
    home_re, home_im = complex_times(home_re, home_im, first_re, -first_im)
    real_part = jnp.einsum("ko,ckis->cois", outer_re, home_re) + jnp.einsum(
        "ko,ckis->cois", outer_im, home_im
    )
    real_part = real_part * (1.0 / length)
    arranged = real_part.reshape(1, 1, chan_local, outer_count, inner_count, rows)
    settled = exchange_both(
        arranged.astype(jnp.bfloat16), ("outer", "inner"), ("outer", "inner"), (3, 4), (0, 1)
    ).astype(arranged.dtype)
    conv = settled.reshape(channels, rows).T
    return (query * (conv + skip_gain[None, :] * mixed)).astype(jnp.bfloat16)


def solution(mesh):
    in_specs = (P(("outer", "inner"), None), P(), P(), P(), P())
    out_specs = P(("outer", "inner"), None)
    return jax.shard_map(
        on_device, mesh=mesh, in_specs=in_specs, out_specs=out_specs, check_vma=False
    )
```

profile of v0, /device:TPU:1, one launch (start us, length us, event | category | flops | bytes accessed | tf_op | source)
XLA Modules:
  0.0 208.0 jit_solution(6457996666671919471)
XLA Ops:
  0.0 1.0 slice.127
  1.0 4.4 %collective-permute-start = (bf16[2,12288]{1,0:T(2,128)(2,1)S(1)}, bf16[2,12288]{1,0:T(2,128)(2,1)S(1)}, u32[]{:S(2)}, u32[]{:S(2)}) collective-permute-start(bf16[2,12288]{1,0:T(2,128)(2,1)S(1)} %slice.127), channel_id=1, source_target_pairs={{0,1},{1,2},{2,3},{3,4},{4,5},{5,6},{6,7},{7,8},{8,9},{9,10},{10,1... | collective-permute-start | bytes 147464 | tf_op jit(solution)/shard_map/ppermute | solution.py:12
  5.4 0.1 fusion.176
  5.4 0.3 fusion.118.clone.5
  5.7 0.1 fusion.184
  5.7 1.3 fusion.284
  7.0 1.9 exponential_bitcast_fusion.15
  9.0 0.6 exponential_bitcast_fusion.12
  9.6 0.6 exponential_bitcast_fusion.14
  10.2 0.6 iota_multiply_fusion.2
  10.8 3.5 %copy.36 = bf16[128,12288]{0,1:T(8,128)(2,1)S(1)} copy(bf16[128,12288]{1,0:T(8,128)(2,1)} %param.5) | data formatting | bytes 6291456 | tf_op args[0]
  14.2 0.0 collective-permute-done
  14.2 2.8 %copy.35 = bf16[2,12288]{0,1:T(8,128)(2,1)} copy(bf16[2,12288]{1,0:T(2,128)(2,1)S(1)} %collective-permute-done) | data formatting | bytes 98304 | tf_op jit(solution)/shard_map/ppermute | solution.py:12
  17.1 4.0 %maximum_convert_fusion = f32[130,12288]{0,1:T(8,128)S(1)} fusion(bf16[128,12288]{0,1:T(8,128)(2,1)S(1)} %copy.36, bf16[2,12288]{0,1:T(8,128)(2,1)} %copy.35), kind=kLoop, calls=%fused_computation.5 | loop fusion | flops 6389760 | bytes 9584640 | tf_op jit(solution)/shard_map/convert_element_type | solution.py:127
  21.1 9.5 %fusion = f32[128,12288]{0,1:T(8,128)S(1)} fusion(f32[130,12288]{0,1:T(8,128)S(1)} %maximum_convert_fusion, f32[12288]{0:T(1024)S(1)} %bitcast.347, f32[12288]{0:T(1024)S(1)} %bitcast.348, f32[12288]{0:T(1024)S(1)} %bitcast.346), kind=kLoop, calls=%fused_computation.1 | loop fusion | flops 7864320 | bytes 25313280 | tf_op jit(solution)/shard_map/add | solution.py:128
  30.7 0.0 copy-start
  30.7 2.7 %copy-done = f32[128,12288]{0,1:T(8,128)} copy-done((f32[128,12288]{0,1:T(8,128)}, f32[128,12288]{0,1:T(8,128)S(1)}, u32[]{:S(2)}) %copy-start) | copy-done | bytes 6291480
  33.4 1.2 fusion.93
  34.5 14.8 %all-to-all-start = ((bf16[256,1,1,16,1,1,128]{6,3,5,4,2,1,0:T(8,128)(2,1)}), bf16[256,1,1,16,1,1,128]{6,3,5,4,2,1,0:T(8,128)(2,1)S(1)}, u32[]{:S(2)}, u32[]{:S(2)}) async-start(bf16[256,1,1,16,1,1,128]{6,3,5,4,2,1,0:T(8,128)(2,1)} %bitcast.5), calls=%async_computation | async-start | bytes 2097152 | tf_op jit(solution)/shard_map/all_to_all | solution.py:33
  49.3 0.7 copy.47
  50.0 0.7 copy.48
  50.8 0.0 copy-done.14
  50.8 0.2 fusion.103
  51.0 3.7 %fusion.110 = (f32[32,16,128]{2,1,0:T(8,128)}, f32[32,16,128]{2,1,0:T(8,128)S(1)}, f32[32,16,128]{2,1,0:T(8,128)S(1)}, f32[32,16,128]{2,1,0:T(8,128)S(1)}, f32[32,16,128]{2,1,0:T(8,128)S(1)}) fusion(s32[32,16]{1,0:T(8,128)S(1)} %iota_add_fusion, s32[128]{0:T(128)S(1)} %iota_multiply_fusion.1), kind=kLoop, calls=%fused_computation.203 | loop fusion | flops 1245184 | bytes 1313280 | tf_op jit(solution)/shard_map/neg | solution.py:108
  54.7 27.0 %all-to-all-done = bf16[256,1,1,16,1,1,128]{6,3,5,4,2,1,0:T(8,128)(2,1)S(1)} async-done(((bf16[256,1,1,16,1,1,128]{6,3,5,4,2,1,0:T(8,128)(2,1)}), bf16[256,1,1,16,1,1,128]{6,3,5,4,2,1,0:T(8,128)(2,1)S(1)}, u32[]{:S(2)}, u32[]{:S(2)}) %all-to-all-start) | async-done | bytes 1048608 | tf_op jit(solution)/shard_map/all_to_all | solution.py:33
  81.7 1.4 fusion.89
  83.1 2.7 %fusion.52 = (bf16[16,32,16,128]{3,1,2,0:T(8,128)(2,1)S(1)}, bf16[16,32,16,128]{3,1,2,0:T(8,128)(2,1)S(1)}) fusion(f32[16,16,128,32]{2,3,1,0:T(8,128)S(1)} %fusion.89, f32[32,16]{0,1:T(8,128)S(1)} %get-tuple-element.179, f32[32,16]{0,1:T(8,128)S(1)} %get-tuple-element.180, bf16[16,16,1,1,16,1,1,128]{7,4,1,0,6,5,3,2:T(8,128)(2,1)S(1)} %bitcast.344), kind=kOutput, calls=%fused_computation.94 | convolution fusion | flops 41950208 | bytes 9441280 | tf_op jit(solution)/shard_map/ko,cois->ckis/dot_general | solution.py:145
  85.8 0.9 fusion.60
  86.7 0.9 fusion.58
  87.7 1.1 fusion.66
  88.8 1.0 fusion.69
  89.8 1.2 fusion.85
  91.0 1.2 fusion.83
  92.2 0.0 copy-start.5
  92.3 0.0 copy-start.6
  92.3 0.0 copy-start.7
  92.3 0.0 copy-start.8
  92.3 0.0 copy-start.9
  92.3 0.0 copy-start.10
  92.3 0.0 copy-start.11
  92.5 1.5 convolution_subtract_fusion.2
  94.0 0.0 copy-done.5
  94.3 56.6 %multiply_subtract_fusion.1 = (bf16[16,32,16,128]{3,2,1,0:T(8,128)(2,1)S(1)}, f32[16,32,16,128]{3,2,1,0:T(8,128)}, f32[16,32,16,128]{3,2,1,0:T(8,128)}, f32[16,32,16,128]{3,2,1,0:T(8,128)}) fusion(f32[16,32,16,128]{3,2,1,0:T(8,128)S(1)} %convolution_subtract_fusion.2, f32[16]{0:T(128)S(1)} %get-tuple-element.175, f32[16]{0:T(128)S(1)} %get-tuple-element.177, ...), kind=kOutput, calls=%fused_computation.107 | convolution fusion | flops 544210944 | bytes 32838656 | tf_op jit(solution)/shard_map/ckjs,sq->ckjq/dot_general | solution.py:79
  150.9 0.9 fusion.116
  151.8 5.8 %multiply_add_fusion.1 = bf16[16,32,16,128]{3,2,1,0:T(8,128)(2,1)S(1)} fusion(f32[16,32,16,128]{3,2,1,0:T(8,128)} %get-tuple-element.178, f32[16,32,16,128]{3,2,1,0:T(8,128)} %get-tuple-element.7, f32[16,32,16,128]{3,2,1,0:T(8,128)S(1)} %convolution_subtract_fusion.2, f32[16,32,16,128]{3,2,1,0:T(8,128)} %get-tuple-element.6), kind=kLoop, calls=%fused_computation.106 | loop fusion | flops 4194304 | bytes 18874368 | tf_op jit(solution)/shard_map/add | solution.py:49
  157.7 0.9 fusion.114
  158.6 0.9 convolution_add_fusion.1
  159.6 0.9 convolution_subtract_fusion.1
  160.5 1.1 fusion.79
  161.7 1.2 fusion.80
  162.8 0.0 copy-start.2
  162.8 0.0 copy-start.3
  162.8 1.5 convolution_subtract_fusion
  164.4 2.6 %subtract_bitcast_fusion = (bf16[16,32,16,128]{3,2,1,0:T(8,128)(2,1)S(1)}, bf16[16,32,16,128]{3,2,1,0:T(8,128)(2,1)S(1)}) fusion(f32[16,32,128,16]{2,3,1,0:T(8,128)S(1)} %convolution_subtract_fusion, f32[32,16]{1,0:T(8,128)S(1)} %copy-done.3, f32[32,16]{1,0:T(8,128)S(1)} %copy-done.2, f32[16,32,128,16]{2,3,1,0:T(8,128)S(1)} %fusion.79, ...), kind=kOutput, calls=%fused_computation.103 | convolution fusion | flops 46140928 | bytes 21499904 | tf_op jit(solution)/shard_map/ji,ckjs->ckis/dot_general | solution.py:109
  167.0 0.0 slice-start
  167.0 0.5 fusion.54
  167.6 0.0 slice-start.1
  167.6 0.0 copy-start.4
  167.6 0.6 fusion.76
  168.2 0.7 copy.51
  168.9 36.7 %all_to_all.10 = bf16[256,1,1,16,1,1,128]{6,3,5,4,2,1,0:T(8,128)(2,1)S(1)} all-to-all(bf16[256,1,1,16,1,1,128]{6,3,5,4,2,1,0:T(8,128)(2,1)S(1)} %bitcast.345), channel_id=1, replica_groups=mesh['outer'=16,'inner'=16] {'outer','inner'}, dimensions={0} | all-to-all | bytes 2097152 | tf_op jit(solution)/shard_map/all_to_all | solution.py:33
  205.6 0.0 copy-done.4
  205.6 0.9 fusion.72
  206.5 1.3 copy.53
  (60 shorter events, 0.2 us)
Async XLA Ops:
  1.0 13.3 %collective-permute-start = (bf16[2,12288]{1,0:T(2,128)(2,1)S(1)}, bf16[2,12288]{1,0:T(2,128)(2,1)S(1)}, u32[]{:S(2)}, u32[]{:S(2)}) collective-permute-start(bf16[2,12288]{1,0:T(2,128)(2,1)S(1)} %slice.127), channel_id=1, source_target_pairs={{0,1},{1,2},{2,3},{3,4},{4,5},{5,6},{6,7},{7,8},{8,9},{9,10},{10,1... | collective-permute-start | bytes 147464 | tf_op jit(solution)/shard_map/ppermute | solution.py:12
  30.7 2.7 %copy-start = (f32[128,12288]{0,1:T(8,128)}, f32[128,12288]{0,1:T(8,128)S(1)}, u32[]{:S(2)}) copy-start(f32[128,12288]{0,1:T(8,128)S(1)} %fusion) | copy-start | bytes 18874372
  33.3 17.5 %copy-start.14 = (s32[16]{0:T(128)S(1)}, s32[16]{0:T(128)}, u32[]{:S(2)}) copy-start(s32[16]{0:T(128)} %iota_multiply_fusion.2) | copy-start | bytes 196
  34.5 47.2 %all-to-all-start = ((bf16[256,1,1,16,1,1,128]{6,3,5,4,2,1,0:T(8,128)(2,1)}), bf16[256,1,1,16,1,1,128]{6,3,5,4,2,1,0:T(8,128)(2,1)S(1)}, u32[]{:S(2)}, u32[]{:S(2)}) async-start(bf16[256,1,1,16,1,1,128]{6,3,5,4,2,1,0:T(8,128)(2,1)} %bitcast.5), calls=%async_computation | async-start | bytes 2097152 | tf_op jit(solution)/shard_map/all_to_all | solution.py:33
  92.2 1.8 copy-start.5
  92.3 1.8 copy-start.6
  92.3 1.8 copy-start.7
  92.3 1.8 copy-start.8
  92.3 1.8 copy-start.9
  92.3 1.8 copy-start.10
  92.3 1.8 copy-start.11
  92.3 1.8 copy-start.12
  92.3 1.8 copy-start.13
  92.3 1.8 copy-start.15
  92.3 1.8 copy-start.16
  92.4 1.8 copy-start.17
  92.4 1.8 copy-start.18
  92.4 1.8 copy-start.19
  92.4 1.8 copy-start.20
  92.4 1.8 copy-start.21
  92.4 1.8 copy-start.22
  92.4 1.8 copy-start.23
  92.4 1.8 copy-start.24
  92.4 1.8 copy-start.25
  92.4 1.8 copy-start.26
  92.5 1.8 copy-start.27
  92.5 1.8 copy-start.28
  92.5 1.8 copy-start.29
  92.5 1.8 copy-start.30
  92.5 1.8 copy-start.31
  159.5 1.0 copy-start.1
  162.8 1.5 copy-start.2
  162.8 1.5 copy-start.3
  167.0 38.5 %slice-start = ((s8[6291456]{0:T(1024)(128)(4,1)}), s8[4194304]{0:T(1024)(128)(4,1)S(1)}, s32[]{:S(2)}) async-start(s8[6291456]{0:T(1024)(128)(4,1)} %bitcast.341), calls=%async_computation.2 | async-start | bytes 8388608
  167.6 38.0 %slice-start.1 = ((s8[6291456]{0:T(1024)(128)(4,1)}), s8[2097152]{0:T(1024)(128)(4,1)S(1)}, s32[]{:S(2)}) async-start(s8[6291456]{0:T(1024)(128)(4,1)} %bitcast.341), calls=%async_computation.3 | async-start | bytes 4194304
  167.6 38.0 %copy-start.4 = (f32[4096]{0:T(1024)S(1)}, f32[4096]{0:T(1024)}, u32[]{:S(2)}) copy-start(f32[4096]{0:T(1024)} %param.9) | copy-start | bytes 49156
where the time goes:
time: 212 us; the launch traced here: 208 us
  matrix products  80 us (38%)
  blocking collectives  36.7 us (17%)
  other arithmetic  29.6 us (14%)
  waiting for transfers between devices  27 us (13%)
  starting transfers between devices  19.2 us (9%)
  local copies, waits for them, and re-layouts  14.7 us (7%)
    dot_general x1, matrix products, middle_segment(): jnp.einsum('ckjs,sq->ckjq', mid_im, local_re)  56.6 us
    all_to_all x1, blocking collectives, exchange_both(): lax.all_to_all(blocks, axis, split_axis=0, concat_axis=0, tiled=True)  36.7 us
    all_to_all x1, waiting for transfers between devices, exchange_both(): lax.all_to_all(blocks, axis, split_axis=0, concat_axis=0, tiled=True)  27 us
    all_to_all x1, starting transfers between devices, exchange_both(): lax.all_to_all(blocks, axis, split_axis=0, concat_axis=0, tiled=True)  14.8 us
    add x1, other arithmetic, on_device(): short_taps[0] * padded[2:] + short_taps[1] * padded[1:-1]  9.54 us
    unnamed x69, local copies, waits for them, and re-layouts  6.3 us
    add x1, other arithmetic, complex_times(): left_re * right_im + left_im * right_re  5.81 us
    ppermute x1, starting transfers between devices, passed_along(): lax.ppermute(value, axis, [(source, source + steps) for source in range(l...  4.36 us
  transfers between devices with their start and end apart: 2, of which 1 were waited for; matrix products, arithmetic and copies ran while one was open for 7% of the time, Pallas kernels for 0%

commit v1 on v0

v1 whole, which is shorter than its diff:
```python
import functools

import jax
import jax.numpy as jnp
from jax import lax
from jax.experimental import pallas as pl
from jax.experimental.pallas import tpu as pltpu
from jax.sharding import PartitionSpec as P

MESH = pl.DeviceIdType.MESH
F32 = jnp.float32
BF16 = jnp.bfloat16
SUB = 8
LANE = 128
GROUP = SUB * LANE
CHUNK = 16


def kernel(dims, proj, taps_in, rates_in, resid_in, skip_in, out, raw, ktm, vtm, qtm, base, taps_n, rate_n, res_n,
           skip_v, taps_t, rtm, dtm, atm, zfin, edge, stg, ctm, hsend, hrecv, send1, recv1, send2, recv2, send3, recv3,
           outb, in_sem, par_sem, out_sem, hs_sem, hr_sem, s1_sem, r1_sem, s2_sem, r2_sem, s3_sem, r3_sem):
    outer_n, inner_n, rows, channels, modes = dims
    groups = channels // GROUP
    chunks = rows // CHUNK
    per_owner = channels // inner_n
    owners_g = GROUP // per_owner
    block = modes * per_owner // LANE
    sub_o = per_owner // LANE
    last = rows - CHUNK
    o = lax.axis_index("outer")
    i = lax.axis_index("inner")
    p = o * inner_n + i
    total = outer_n * inner_n
    nxt, prv = lax.rem(p + 1, total), lax.rem(p + total - 1, total)
    nxt_id = (nxt // inner_n, lax.rem(nxt, inner_n))
    prv_id = (prv // inner_n, lax.rem(prv, inner_n))

    bar = pltpu.get_barrier_semaphore()
    for k in range(1, inner_n):
        pl.semaphore_signal(bar, inc=1, device_id=(o, lax.rem(i + k, inner_n)), device_id_type=MESH)
    for k in range(1, outer_n):
        pl.semaphore_signal(bar, inc=1, device_id=(lax.rem(o + k, outer_n), i), device_id_type=MESH)
    pl.semaphore_signal(bar, inc=1, device_id=nxt_id, device_id_type=MESH)
    pl.semaphore_signal(bar, inc=1, device_id=prv_id, device_id_type=MESH)

    tail_cp = pltpu.make_async_copy(proj.at[pl.ds(last, CHUNK), :], raw.at[pl.ds(last, CHUNK), :], in_sem.at[3 * groups])
    tail_cp.start()
    par_cps = [pltpu.make_async_copy(a, b, par_sem.at[n]) for n, (a, b) in enumerate(
        ((taps_in, taps_n), (rates_in, rate_n), (resid_in, res_n), (skip_in, skip_v)))]
    for cp in par_cps:
        cp.start()

    def in_copy(f, g):
        cols = pl.ds((f * groups + g) * GROUP, GROUP)
        return pltpu.make_async_copy(proj.at[pl.ds(0, last), cols], raw.at[pl.ds(0, last), cols],
                                     in_sem.at[f * groups + g])

    for g in range(groups):
        in_copy(1, g).start()
        in_copy(2, g).start()
    for g in range(groups):
        in_copy(0, g).start()
    tms = (qtm, ktm, vtm)

    def relay_chunk(f, g, c):
        for s in range(SUB):
            col = (f * groups + g) * GROUP + s * LANE
            v = raw[pl.ds(pl.multiple_of(c * CHUNK, CHUNK), CHUNK), pl.ds(col, LANE)].astype(F32)
            tms[f][g, pl.ds(c * (CHUNK * SUB) + s, CHUNK, stride=SUB), :] = v

    tail_cp.wait()
    for f in range(3):
        for g in range(groups):
            relay_chunk(f, g, chunks - 1)
            hsend[f * groups + g] = tms[f][g, pl.ds((rows - 2) * SUB, 2 * SUB), :].astype(BF16)

    for cp in par_cps:
        cp.wait()
    for fg in range(3 * groups):
        for s in range(SUB):
            taps_t[pl.ds(fg * 3 * SUB + s, 3, stride=SUB), :] = taps_n[:, pl.ds(fg * GROUP + s * LANE, LANE)]
    for g in range(groups):
        for s in range(SUB):
            cols = pl.ds(g * GROUP + s * LANE, LANE)
            r = rate_n[:, cols]
            rtm[g, pl.ds(s, modes, stride=SUB), :] = r
            dtm[g, pl.ds(s, modes, stride=SUB), :] = jnp.exp(-r)
            atm[g, pl.ds(s, modes, stride=SUB), :] = res_n[:, cols] * jnp.sqrt(2.0 * r)

    def tap(f, g):
        return [taps_t[pl.ds(((f * groups + g) * 3 + j) * SUB, SUB), :] for j in range(3)]

    def mode(ref, g, m):
        return ref[g, pl.ds(m * SUB, SUB), :]

    def tok(ref, g, t):
        return ref[g, pl.ds(pl.multiple_of(t * SUB, SUB), SUB), :]

    def tree(vals):
        vals = list(vals)
        while len(vals) > 1:
            vals = [a + b for a, b in zip(vals[::2], vals[1::2])] + (vals[-1:] if len(vals) % 2 else [])
        return vals[0]

    def recur(g):
        d = [mode(dtm, g, m) for m in range(modes)]
        tk, tv = tap(1, g), tap(2, g)
        sk = skip_v[pl.ds(g * SUB, SUB), :]

        def body(t2, carry):
            z = list(carry[:modes])
            k1, k2, v1, v2 = carry[modes:]
            xs = []
            for u in range(2):
                k0, v0 = tok(ktm, g, t2 * 2 + u), tok(vtm, g, t2 * 2 + u)
                xs.append((tk[0] * k0 + tk[1] * k1 + tk[2] * k2) * (tv[0] * v0 + tv[1] * v1 + tv[2] * v2))
                k1, k2, v1, v2 = k0, k1, v0, v1
            accs = [[xs[0] * sk, None, None, None], [xs[1] * sk, None, None, None]]
            for m in range(modes):
                a = mode(atm, g, m)
                for u in range(2):
                    z[m] = d[m] * z[m] + xs[u]
                    term = a * z[m]
                    old = accs[u][m % 4]
                    accs[u][m % 4] = term if old is None else old + term
            for u in range(2):
                base[g, pl.ds(pl.multiple_of((t2 * 2 + u) * SUB, SUB), SUB), :] = tree(accs[u])
            return (*z, k1, k2, v1, v2)

        zero = jnp.zeros((SUB, LANE), F32)
        init = (*([zero] * modes), tok(ktm, g, 1), tok(ktm, g, 0), tok(vtm, g, 1), tok(vtm, g, 0))
        done = lax.fori_loop(1, rows // 2, body, init)
        for m in range(modes):
            zfin[g, pl.ds(m * SUB, SUB), :] = done[m]

    halo = pltpu.make_async_remote_copy(src_ref=hsend, dst_ref=hrecv, send_sem=hs_sem, recv_sem=hr_sem,
                                        device_id=nxt_id, device_id_type=MESH)
    for g in range(groups):
        if g == groups // 2:
            pl.semaphore_wait(bar, inner_n + outer_n)
            halo.start()
        for f in (1, 2):
            in_copy(f, g).wait()

        def relay(c, _):
            relay_chunk(1, g, c)
            relay_chunk(2, g, c)
            return 0

        lax.fori_loop(0, chunks - 1, relay, 0)
        recur(g)

    halo.wait_recv()
    first = p == 0

    def halo_of(f, g):
        both = hrecv[f * groups + g].astype(F32)
        both = jnp.where(first, jnp.zeros_like(both), both)
        return both[:SUB], both[SUB:]

    for g in range(groups):
        feats = []
        for f in (1, 2):
            h2, h1 = halo_of(f, g)
            t0, t1, t2 = tap(f, g)
            e0, e1 = tok(tms[f], g, 0), tok(tms[f], g, 1)
            feats.append((t0 * e0 + t1 * h1 + t2 * h2, t0 * e1 + t1 * e0 + t2 * h1))
        x0, x1 = feats[0][0] * feats[1][0], feats[0][1] * feats[1][1]
        edge[g, pl.ds(0, SUB), :] = x0
        edge[g, pl.ds(SUB, SUB), :] = x1
        for m in range(modes):
            state = mode(zfin, g, m) + jnp.exp(-(rows - 2.0) * mode(rtm, g, m)) * (mode(dtm, g, m) * x0 + x1)
            stg[g, pl.ds(m, SUB, stride=modes), :] = state
        for w in range(owners_g):
            j = g * owners_g + w
            val = stg[g, pl.ds(w * block, block), :].astype(BF16)

            @pl.when(j == i)
            def _():
                recv1[j] = val

            @pl.when(j != i)
            def _():
                send1[j] = val
                pltpu.make_async_remote_copy(src_ref=send1.at[j], dst_ref=recv1.at[i], send_sem=s1_sem.at[j],
                                             recv_sem=r1_sem.at[i], device_id=(o, j), device_id_type=MESH).start()

    for g in range(groups):
        in_copy(0, g).wait()

        def relay_q(c, _):
            relay_chunk(0, g, c)
            return 0

        lax.fori_loop(0, chunks - 1, relay_q, 0)
        t0, t1, t2 = tap(0, g)
        h2, h1 = halo_of(0, g)

        def gate(t, carry):
            q1, q2 = carry
            for u in range(2):
                q0 = tok(qtm, g, t * 2 + u)
                qtm[g, pl.ds(pl.multiple_of((t * 2 + u) * SUB, SUB), SUB), :] = t0 * q0 + t1 * q1 + t2 * q2
                q1, q2 = q0, q1
            return q1, q2

        lax.fori_loop(0, rows // 2, gate, (h1, h2))

    for n in range(inner_n):
        @pl.when(n != i)
        def _():
            pltpu.make_async_remote_copy(src_ref=send1.at[n], dst_ref=recv1.at[n], send_sem=s1_sem.at[n],
                                         recv_sem=r1_sem.at[n], device_id=(o, n), device_id_type=MESH).wait_recv()

    def own_rate(w):
        return rate_n[:, pl.ds(pl.multiple_of(i * per_owner + w * LANE, LANE), LANE)]

    own = jnp.concatenate([own_rate(w) for w in range(sub_o)], axis=0)
    dec_in = jnp.exp(-float(rows) * own)
    dec_out = jnp.exp(-float(rows * inner_n) * own)
    run = recv1[0].astype(F32)
    for n in range(1, inner_n):
        run = dec_in * run + recv1[n].astype(F32)
    send2[...] = run.astype(BF16)
    for k in range(1, outer_n):
        @pl.when(o + k < outer_n)
        def _():
            pltpu.make_async_remote_copy(src_ref=send2, dst_ref=recv2.at[o], send_sem=s2_sem.at[k],
                                         recv_sem=r2_sem.at[o], device_id=(o + k, i), device_id_type=MESH).start()

    for g in range(groups):
        x0, x1 = edge[g, pl.ds(0, SUB), :], edge[g, pl.ds(SUB, SUB), :]
        sk = skip_v[pl.ds(g * SUB, SUB), :]
        lead = tree([mode(atm, g, m) * jnp.exp(mode(rtm, g, m)) for m in range(modes)])
        base[g, pl.ds(0, SUB), :] = sk * x0 - x1 * lead
        base[g, pl.ds(SUB, SUB), :] = sk * x1
        for m in range(modes):
            r = mode(rtm, g, m)
            zfin[g, pl.ds(m * SUB, SUB), :] = jnp.exp(r) * x0 + jnp.exp(2.0 * r) * x1

    def add_outer(n, acc):
        pltpu.make_async_remote_copy(src_ref=send2, dst_ref=recv2.at[n], send_sem=s2_sem.at[0],
                                     recv_sem=r2_sem.at[n], device_id=(n, i), device_id_type=MESH).wait_recv()
        return dec_out * acc + recv2[n].astype(F32)

    run = lax.fori_loop(0, o, add_outer, jnp.zeros((block, LANE), F32))
    for n in range(inner_n):
        send3[n] = run.astype(BF16)
        if n < inner_n - 1:
            run = dec_in * run + recv1[n].astype(F32)
    recv3[i] = send3[i]
    for k in range(1, inner_n):
        j = lax.rem(i + k, inner_n)
        pltpu.make_async_remote_copy(src_ref=send3.at[j], dst_ref=recv3.at[i], send_sem=s3_sem.at[j],
                                     recv_sem=r3_sem.at[i], device_id=(o, j), device_id_type=MESH).start()

    for g in range(groups):
        for w in range(owners_g):
            n = g * owners_g + w

            @pl.when(n != i)
            def _():
                pltpu.make_async_remote_copy(src_ref=send3.at[n], dst_ref=recv3.at[n], send_sem=s3_sem.at[n],
                                             recv_sem=r3_sem.at[n], device_id=(o, n), device_id_type=MESH).wait_recv()

            got = recv3[n].astype(F32)
            for u in range(sub_o):
                ctm[g, pl.ds(w * sub_o + u, modes, stride=SUB), :] = got[u * modes:(u + 1) * modes]
        d = [mode(dtm, g, m) for m in range(modes)]
        init = tuple(mode(atm, g, m) * (mode(ctm, g, m) + mode(zfin, g, m)) for m in range(modes))

        def apply(t2, carry):
            s = list(carry)
            for u in range(2):
                s = [d[m] * s[m] for m in range(modes)]
                where = pl.ds(pl.multiple_of((t2 * 2 + u) * SUB, SUB), SUB)
                base[g, where, :] = qtm[g, where, :] * (base[g, where, :] + tree(s))
            return tuple(s)

        lax.fori_loop(0, rows // 2, apply, init)

        def settle(c, _):
            for s in range(SUB):
                v = base[g, pl.ds(c * (CHUNK * SUB) + s, CHUNK, stride=SUB), :].astype(BF16)
                outb[pl.ds(pl.multiple_of(c * CHUNK, CHUNK), CHUNK), pl.ds(g * GROUP + s * LANE, LANE)] = v
            return 0

        lax.fori_loop(0, chunks, settle, 0)
        cols = pl.ds(g * GROUP, GROUP)
        pltpu.make_async_copy(outb.at[:, cols], out.at[:, cols], out_sem.at[g]).start()

    halo.wait_send()
    for n in range(inner_n):
        @pl.when(n != i)
        def _():
            for src, sem in ((send1, s1_sem), (send3, s3_sem)):
                pltpu.make_async_remote_copy(src_ref=src.at[n], dst_ref=src.at[n], send_sem=sem.at[n],
                                             recv_sem=sem.at[n], device_id=(o, n), device_id_type=MESH).wait_send()
    for k in range(1, outer_n):
        @pl.when(o + k < outer_n)
        def _():
            pltpu.make_async_remote_copy(src_ref=send2, dst_ref=send2, send_sem=s2_sem.at[k], recv_sem=s2_sem.at[k],
                                         device_id=(o, i), device_id_type=MESH).wait_send()
    for g in range(groups):
        cols = pl.ds(g * GROUP, GROUP)
        pltpu.make_async_copy(outb.at[:, cols], out.at[:, cols], out_sem.at[g]).wait()


def solution(mesh):
    outer_n, inner_n = mesh.shape["outer"], mesh.shape["inner"]

    def on_device(projected, short_taps, rates, residues, skip_gain):
        rows, width = projected.shape
        channels, modes = rates.shape
        groups = channels // GROUP
        per_owner = channels // inner_n
        block = modes * per_owner // LANE
        any_spec = pl.BlockSpec(memory_space=pl.ANY)
        dma = pltpu.SemaphoreType.DMA
        tm = pltpu.VMEM((groups, rows * SUB, LANE), F32)
        pm = pltpu.VMEM((groups, modes * SUB, LANE), F32)
        return pl.pallas_call(
            functools.partial(kernel, (outer_n, inner_n, rows, channels, modes)),
            out_shape=jax.ShapeDtypeStruct((rows, channels), BF16),
            in_specs=[any_spec] * 5,
            out_specs=any_spec,
            scratch_shapes=[
                pltpu.VMEM((rows, width), BF16), tm, tm, tm, tm,
                pltpu.VMEM((3, width), F32), pltpu.VMEM((modes, channels), F32), pltpu.VMEM((modes, channels), F32),
                pltpu.VMEM((groups * SUB, LANE), F32), pltpu.VMEM((3 * 3 * groups * SUB, LANE), F32),
                pm, pm, pm, pm,
                pltpu.VMEM((groups, 2 * SUB, LANE), F32), pm, pm,
                pltpu.VMEM((3 * groups, 2 * SUB, LANE), BF16), pltpu.VMEM((3 * groups, 2 * SUB, LANE), BF16),
                pltpu.VMEM((inner_n, block, LANE), BF16), pltpu.VMEM((inner_n, block, LANE), BF16),
                pltpu.VMEM((block, LANE), BF16), pltpu.VMEM((outer_n, block, LANE), BF16),
                pltpu.VMEM((inner_n, block, LANE), BF16), pltpu.VMEM((inner_n, block, LANE), BF16),
                pltpu.VMEM((rows, channels), BF16),
                dma((3 * groups + 1,)), dma((4,)), dma((groups,)), dma, dma,
                dma((inner_n,)), dma((inner_n,)), dma((outer_n,)), dma((outer_n,)), dma((inner_n,)), dma((inner_n,)),
            ],
            compiler_params=pltpu.CompilerParams(collective_id=0, has_side_effects=True,
                                                 vmem_limit_bytes=48 * 1024 * 1024),
            name="modal_scan",
        )(projected, short_taps, rates.T, residues.T, skip_gain.reshape(groups * SUB, LANE))

    return jax.shard_map(
        on_device, mesh=mesh,
        in_specs=(P(("outer", "inner"), None), P(), P(), P(), P()),
        out_specs=P(("outer", "inner"), None), check_vma=False,
    )
```

time: 212 us -> 42.3 us (0.20)
  the two profiles are of different devices: /device:TPU:1 before, /device:TPU:20 now
where the time goes in v1:
time: 42.3 us; the launch traced here: 42.1 us
  Pallas kernels  35.7 us (84%)
  local copies, waits for them, and re-layouts  6.4 us (15%)
    pallas_call x1, Pallas kernels, on_device(): pl.pallas_call(functools.partial(kernel, (outer_n, inner_n, rows, channel...  35.7 us
    unnamed x11, local copies, waits for them, and re-layouts  6.4 us

profile of v1, /device:TPU:20, one launch (start us, length us, event | category | flops | bytes accessed | tf_op | source)
XLA Modules:
  0.0 42.1 jit_solution(7158658475615099565)
XLA Ops:
  0.0 0.0 copy-start
  0.0 1.9 %copy-done = bf16[128,12288]{1,0:T(8,128)(2,1)S(1)} copy-done((bf16[128,12288]{1,0:T(8,128)(2,1)S(1)}, bf16[128,12288]{1,0:T(8,128)(2,1)}, u32[]{:S(2)}) %copy-start) | copy-done | bytes 3145752
  1.9 0.0 copy-start.1
  1.9 0.9 %copy-done.1 = f32[4096,16]{0,1:T(8,128)S(1)} copy-done((f32[4096,16]{0,1:T(8,128)S(1)}, f32[4096,16]{0,1:T(8,128)}, u32[]{:S(2)}) %copy-start.1) | copy-done | bytes 262168
  2.8 0.0 copy-start.2
  2.8 0.9 %copy-done.2 = f32[4096,16]{0,1:T(8,128)S(1)} copy-done((f32[4096,16]{0,1:T(8,128)S(1)}, f32[4096,16]{0,1:T(8,128)}, u32[]{:S(2)}) %copy-start.2) | copy-done | bytes 262168
  3.8 0.0 copy-start.3
  3.8 0.9 %copy-done.3 = f32[3,12288]{1,0:T(4,128)S(1)} copy-done((f32[3,12288]{1,0:T(4,128)S(1)}, f32[3,12288]{1,0:T(4,128)}, u32[]{:S(2)}) %copy-start.3) | copy-done | bytes 147480
  4.7 0.0 copy-start.4
  4.7 0.7 %copy-done.4 = f32[4096]{0:T(1024)S(1)} copy-done((f32[4096]{0:T(1024)S(1)}, f32[4096]{0:T(1024)}, u32[]{:S(2)}) %copy-start.4) | copy-done | bytes 16408
  5.4 35.7 %modal_scan.1 = bf16[128,4096]{1,0:T(8,128)(2,1)S(1)} custom-call(bf16[128,12288]{1,0:T(8,128)(2,1)S(1)} %copy-done, f32[3,12288]{1,0:T(4,128)S(1)} %copy-done.3, f32[16,4096]{1,0:T(8,128)S(1)} %bitcast.3, f32[16,4096]{1,0:T(8,128)S(1)} %bitcast.4, f32[32,128]{1,0:T(8,128)S(1)} %bitcast.5), custom_call_target="tpu_custom_call" | custom-call | tf_op jit(solution)/shard_map/modal_scan/pallas_call | solution.py:322
  41.1 1.0 %copy.7 = bf16[128,4096]{1,0:T(8,128)(2,1)} copy(bf16[128,4096]{1,0:T(8,128)(2,1)S(1)} %modal_scan.1) | data formatting | bytes 2097152
Async XLA Ops:
  0.0 1.9 %copy-start = (bf16[128,12288]{1,0:T(8,128)(2,1)S(1)}, bf16[128,12288]{1,0:T(8,128)(2,1)}, u32[]{:S(2)}) copy-start(bf16[128,12288]{1,0:T(8,128)(2,1)} %proj.1) | copy-start | bytes 9437188
  1.9 0.9 %copy-start.1 = (f32[4096,16]{0,1:T(8,128)S(1)}, f32[4096,16]{0,1:T(8,128)}, u32[]{:S(2)}) copy-start(f32[4096,16]{0,1:T(8,128)} %param.7) | copy-start | bytes 786436
  2.8 0.9 %copy-start.2 = (f32[4096,16]{0,1:T(8,128)S(1)}, f32[4096,16]{0,1:T(8,128)}, u32[]{:S(2)}) copy-start(f32[4096,16]{0,1:T(8,128)} %param.8) | copy-start | bytes 786436
  3.8 0.9 %copy-start.3 = (f32[3,12288]{1,0:T(4,128)S(1)}, f32[3,12288]{1,0:T(4,128)}, u32[]{:S(2)}) copy-start(f32[3,12288]{1,0:T(4,128)} %taps_in.1) | copy-start | bytes 442372
  4.7 0.7 %copy-start.4 = (f32[4096]{0:T(1024)S(1)}, f32[4096]{0:T(1024)}, u32[]{:S(2)}) copy-start(f32[4096]{0:T(1024)} %param.9) | copy-start | bytes 49156

commit v2 on v1

--- a/solution.py
+++ b/solution.py
@@ -339,7 +339,7 @@
                 dma((inner_n,)), dma((inner_n,)), dma((outer_n,)), dma((outer_n,)), dma((inner_n,)), dma((inner_n,)),
             ],
             compiler_params=pltpu.CompilerParams(collective_id=0, has_side_effects=True,
-                                                 vmem_limit_bytes=48 * 1024 * 1024),
+                                                 vmem_limit_bytes=60 * 1024 * 1024),
             name="modal_scan",
         )(projected, short_taps, rates.T, residues.T, skip_gain.reshape(groups * SUB, LANE))
 

time: 42.3 us -> 39.6 us (0.936)
  local copies, waits for them, and re-layouts: 6.4 us -> 2.29 us
  Pallas kernels: 35.7 us -> 37.1 us
    unnamed x11 -> x1, local copies, waits for them, and re-layouts: 6.4 us -> 2.29 us
    pallas_call x1, Pallas kernels: 35.7 us -> 37.1 us  [on_device(): pl.pallas_call(functools.partial(kernel, (outer_n, inner_n, rows, channel...]
where the time goes in v2:
time: 39.6 us; the launch traced here: 39.4 us
  Pallas kernels  37.1 us (94%)
  local copies, waits for them, and re-layouts  2.29 us (6%)
    pallas_call x1, Pallas kernels, on_device(): pl.pallas_call(functools.partial(kernel, (outer_n, inner_n, rows, channel...  37.1 us
    unnamed x1, local copies, waits for them, and re-layouts  2.29 us

profile of v2, /device:TPU:20, one launch (start us, length us, event | category | flops | bytes accessed | tf_op | source)
XLA Modules:
  0.0 39.4 jit_solution(805356107350450765)
XLA Ops:
  0.0 37.1 %modal_scan.1 = bf16[128,4096]{1,0:T(8,128)(2,1)} custom-call(bf16[128,12288]{1,0:T(8,128)(2,1)} %proj.1, f32[3,12288]{1,0:T(4,128)} %taps_in.1, f32[16,4096]{1,0:T(8,128)} %bitcast.3, f32[16,4096]{1,0:T(8,128)} %bitcast.4, f32[32,128]{1,0:T(8,128)} %bitcast.5), custom_call_target="tpu_custom_call" | custom-call | tf_op jit(solution)/shard_map/modal_scan/pallas_call | solution.py:322
  37.1 2.3 %copy.7 = bf16[128,4096]{1,0:T(8,128)(2,1)} copy(bf16[128,4096]{1,0:T(8,128)(2,1)} %modal_scan.1) | data formatting | bytes 2097152

commit v3 on v2

v3 whole, which is shorter than its diff:
```python
import functools

import jax
import jax.numpy as jnp
from jax import lax
from jax.experimental import pallas as pl
from jax.experimental.pallas import tpu as pltpu
from jax.sharding import PartitionSpec as P

MESH = pl.DeviceIdType.MESH
F32 = jnp.float32
BF16 = jnp.bfloat16
SUB = 8
LANE = 128
GROUP = SUB * LANE
CHUNK = 16
RING = 8


def kernel(dims, proj, taps_in, rates_in, resid_in, skip_in, out, raw, ktmp, vtmp, ktmp2, vtmp2, ttmp, qtm, xs, base, taps_n,
           rate_n, res_n, skip_v, taps_t, rtm, dtm, d16, atm, ztm, ends, edge, head, stg, ctm, pre, powr, hsend, hrecv,
           send1, recv1, send2, recv2, send3, recv3, ytmp, ytmp2, outb, in_sem, par_sem, out_sem, hs_sem, hr_sem, s1_sem,
           r1_sem, s2_sem, r2_sem, s3_sem, r3_sem):
    outer_n, inner_n, rows, channels, modes = dims
    groups = channels // GROUP
    chunks = rows // CHUNK
    n1 = channels // LANE
    total = outer_n * inner_n
    n2 = total // n1
    last = rows - CHUNK
    p = lax.axis_index("outer") * inner_n + lax.axis_index("inner")
    e = lax.rem(p, n1)
    h = p // n1
    far = lax.rem(p, RING) == RING - 1
    near = lax.rem(p, RING) != 0

    def dev(r):
        return (r // inner_n, lax.rem(r, inner_n))

    def mate(n):
        return dev(h * n1 + n)

    def ring_order():
        for dz in (4, 3, 5, 2, 6, 1, 7, 0):
            for hi in range(n1 // RING):
                if dz or hi:
                    yield lax.rem(e // RING + hi, n1 // RING) * RING + lax.rem(lax.rem(e, RING) + dz, RING)

    def remote(src, dst, ssem, rsem, to):
        return pltpu.make_async_remote_copy(src_ref=src, dst_ref=dst, send_sem=ssem, recv_sem=rsem, device_id=to,
                                            device_id_type=MESH)

    kv = pl.ds(channels, 2 * channels)
    tails = [pltpu.make_async_copy(proj.at[pl.ds(last, CHUNK), c], raw.at[pl.ds(last, CHUNK), c], in_sem.at[3 * groups + n])
             for n, c in enumerate((kv, pl.ds(0, channels)))]
    tails[0].start()
    par_cps = [pltpu.make_async_copy(a, b, par_sem.at[n]) for n, (a, b) in enumerate(
        ((rates_in, rate_n), (taps_in, taps_n), (resid_in, res_n), (skip_in, skip_v)))]
    par_cps[0].start()
    par_cps[1].start()

    def in_copy(f, g):
        cols = pl.ds((f * groups + g) * GROUP, GROUP)
        return pltpu.make_async_copy(proj.at[pl.ds(0, last), cols], raw.at[pl.ds(0, last), cols],
                                     in_sem.at[f * groups + g])

    for g in range(groups):
        in_copy(1, g).start()
        in_copy(2, g).start()
    par_cps[2].start()
    par_cps[3].start()
    tails[1].start()
    for g in range(groups):
        in_copy(0, g).start()

    bar = pltpu.get_barrier_semaphore()
    nxt, prv = dev(lax.rem(p + 1, total)), dev(lax.rem(p + total - 1, total))
    for to in (nxt, prv):
        pl.semaphore_signal(bar, inc=1, device_id=to, device_id_type=MESH)
    for k in range(1, n2):
        pl.semaphore_signal(bar, inc=1, device_id=dev(lax.rem(h + k, n2) * n1 + e), device_id_type=MESH)
    for n in ring_order():
        pl.semaphore_signal(bar, inc=1, device_id=mate(n), device_id_type=MESH)

    def relay(dst, row, f, g, c):
        for s in range(SUB):
            col = (f * groups + g) * GROUP + s * LANE
            v = raw[pl.ds(pl.multiple_of(c * CHUNK, CHUNK), CHUNK), pl.ds(col, LANE)].astype(F32)
            dst[pl.ds(row + s, CHUNK, stride=SUB), :] = v

    def tail_of(f):
        for g in range(groups):
            relay(ttmp.at[f * groups + g], 0, f, g, chunks - 1)
            hsend[f * groups + g] = ttmp[f * groups + g, pl.ds((CHUNK - 2) * SUB, 2 * SUB), :].astype(BF16)

    tails[0].wait()
    tail_of(1)
    tail_of(2)
    kv_blocks, q_blocks = pl.ds(groups, 2 * groups), pl.ds(0, groups)
    halo = remote(hsend.at[kv_blocks], hrecv.at[kv_blocks], hs_sem.at[0], hr_sem.at[0], nxt)
    halo_q = remote(hsend.at[q_blocks], hrecv.at[q_blocks], hs_sem.at[1], hr_sem.at[1], nxt)

    def send_halo():
        pl.semaphore_wait(bar, n1 + n2)
        halo.start()

    pl.when(far)(send_halo)

    par_cps[0].wait()
    par_cps[1].wait()
    for f in (1, 2):
        for g in range(groups):
            fg = f * groups + g
            for s in range(SUB):
                taps_t[pl.ds(fg * 3 * SUB + s, 3, stride=SUB), :] = taps_n[:, pl.ds(fg * GROUP + s * LANE, LANE)]
    for g in range(groups):
        for s in range(SUB):
            rtm[g, pl.ds(s, modes, stride=SUB), :] = rate_n[:, pl.ds(g * GROUP + s * LANE, LANE)]
        r = rtm[g]
        dtm[g] = jnp.exp(-r)
        d16[g] = jnp.exp(-float(CHUNK) * r)

    def tap(f, g):
        return [taps_t[pl.ds(((f * groups + g) * 3 + j) * SUB, SUB), :] for j in range(3)]

    def mode(ref, g, m):
        return ref[g, pl.ds(m * SUB, SUB), :]

    def at(t):
        return pl.ds(pl.multiple_of(t * SUB, SUB), SUB)

    def tree(vals):
        vals = list(vals)
        while len(vals) > 1:
            vals = [a + b for a, b in zip(vals[::2], vals[1::2])] + (vals[-1:] if len(vals) % 2 else [])
        return vals[0]

    zero = jnp.zeros((SUB, LANE), F32)

    def states(g):
        d = [mode(dtm, g, m) for m in range(modes)]
        tk, tv = tap(1, g), tap(2, g)
        relay(ktmp, 0, 1, g, 0)
        relay(vtmp, 0, 2, g, 0)
        head[g, pl.ds(0, 2 * SUB), :] = ktmp[pl.ds(0, 2 * SUB), :]
        head[g, pl.ds(2 * SUB, 2 * SUB), :] = vtmp[pl.ds(0, 2 * SUB), :]
        for m in range(modes):
            ztm[g, pl.ds(m * SUB, SUB), :] = zero

        def chunk(c, bufs, spare, carry):
            ahead = jnp.minimum(c + 1, chunks - 1)
            relay(spare[0], 0, 1, g, ahead)
            relay(spare[1], 0, 2, g, ahead)
            k1, k2, v1, v2 = carry
            u = [None] * modes
            for t in range(CHUNK):
                k0, v0 = bufs[0][pl.ds(t * SUB, SUB), :], bufs[1][pl.ds(t * SUB, SUB), :]
                x = (tk[0] * k0 + tk[1] * k1 + tk[2] * k2) * (tv[0] * v0 + tv[1] * v1 + tv[2] * v2)
                if t < 2:
                    x = jnp.where(c == 0, zero, x)
                k1, k2, v1, v2 = k0, k1, v0, v1
                xs[g, at(c * CHUNK + t), :] = x
                u = [x if u[m] is None else d[m] * u[m] + x for m in range(modes)]
            for m in range(modes):
                ends[g, at(c * modes + m), :] = u[m]
                ztm[g, pl.ds(m * SUB, SUB), :] = mode(d16, g, m) * mode(ztm, g, m) + u[m]
            return k1, k2, v1, v2

        def pair(j, carry):
            carry = chunk(2 * j, (ktmp, vtmp), (ktmp2, vtmp2), carry)
            return chunk(2 * j + 1, (ktmp2, vtmp2), (ktmp, vtmp), carry)

        lax.fori_loop(0, chunks // 2, pair, (zero, zero, zero, zero))

    first = p == 0

    def halo_of(f, g):
        both = hrecv[f * groups + g].astype(F32)
        both = jnp.where(first, jnp.zeros_like(both), both)
        return both[:SUB], both[SUB:]

    def emit(g):
        feats = []
        for n, f in enumerate((1, 2)):
            h2, h1 = halo_of(f, g)
            t0, t1, t2 = tap(f, g)
            e0, e1 = head[g, pl.ds(2 * n * SUB, SUB), :], head[g, pl.ds((2 * n + 1) * SUB, SUB), :]
            feats.append((t0 * e0 + t1 * h1 + t2 * h2, t0 * e1 + t1 * e0 + t2 * h1))
        x0, x1 = feats[0][0] * feats[1][0], feats[0][1] * feats[1][1]
        edge[g, pl.ds(0, SUB), :] = x0
        edge[g, pl.ds(SUB, SUB), :] = x1
        for m in range(modes):
            state = mode(ztm, g, m) + jnp.exp(-(rows - 2.0) * mode(rtm, g, m)) * (mode(dtm, g, m) * x0 + x1)
            stg[pl.ds(g * SUB * modes + m, SUB, stride=modes), :] = state
        for s in range(SUB):
            n = g * SUB + s
            send1[n] = stg[pl.ds(n * modes, modes), :].astype(BF16)
        for s in range(SUB):
            n = g * SUB + s

            @pl.when(n == e)
            def _():
                recv1[n] = send1[n]

            @pl.when(n != e)
            def _():
                remote(send1.at[n], recv1.at[e], s1_sem.at[n], r1_sem.at[e], mate(n)).start()

    early = groups - 1
    for g in range(groups):
        for f in (1, 2):
            in_copy(f, g).wait()
        states(g)
        if g == (groups - 1) // 2:
            pl.when(jnp.logical_not(far))(send_halo)
        if g == early - 1:
            @pl.when(near)
            def _():
                halo.wait_recv()
                for n in range(early):
                    emit(n)

    def rest():
        halo.wait_recv()
        for n in range(early):
            emit(n)

    if early:
        pl.when(jnp.logical_not(near))(rest)
    else:
        halo.wait_recv()
    emit(groups - 1)

    tails[1].wait()
    tail_of(0)
    halo_q.start()
    par_cps[2].wait()
    par_cps[3].wait()
    for g in range(groups):
        for s in range(SUB):
            taps_t[pl.ds(g * 3 * SUB + s, 3, stride=SUB), :] = taps_n[:, pl.ds(g * GROUP + s * LANE, LANE)]
            cols = pl.ds(g * GROUP + s * LANE, LANE)
            atm[g, pl.ds(s, modes, stride=SUB), :] = res_n[:, cols] * jnp.sqrt(2.0 * rate_n[:, cols])
    for g in range(groups):
        in_copy(0, g).wait()
        t0, t1, t2 = tap(0, g)

        def gate(c, bufs, spare, carry):
            relay(spare, 0, 0, g, jnp.minimum(c + 1, chunks - 1))
            q1, q2 = carry
            for t in range(CHUNK):
                q0 = bufs[pl.ds(t * SUB, SUB), :]
                qtm[g, at(c * CHUNK + t), :] = t0 * q0 + t1 * q1 + t2 * q2
                q1, q2 = q0, q1
            return q1, q2

        def gates(j, carry):
            return gate(2 * j + 1, ktmp2, ktmp, gate(2 * j, ktmp, ktmp2, carry))

        relay(ktmp, 0, 0, g, 0)
        lax.fori_loop(0, chunks // 2, gates, (zero, zero))

    own = rate_n[:, pl.ds(pl.multiple_of(e * LANE, LANE), LANE)]
    dec_in = jnp.exp(-float(rows) * own)
    dec_out = jnp.exp(-float(rows * n1) * own)
    run = jnp.zeros((modes, LANE), F32)
    for n in range(n1):
        pre[n] = run

        @pl.when(n != e)
        def _():
            remote(send1.at[n], recv1.at[n], s1_sem.at[n], r1_sem.at[n], mate(n)).wait_recv()

        run = dec_in * run + recv1[n].astype(F32)
    send2[...] = run.astype(BF16)
    for k in range(n2 - 1, 0, -1):
        @pl.when(h + k < n2)
        def _():
            remote(send2, recv2.at[h], s2_sem.at[k], r2_sem.at[h], dev((h + k) * n1 + e)).start()

    power = jnp.ones((modes, LANE), F32)
    for n in range(n1):
        powr[n] = power
        power = power * dec_in

    def local(g):
        d = [mode(dtm, g, m) for m in range(modes)]
        a = [mode(atm, g, m) for m in range(modes)]
        taps = []
        for j in range(CHUNK):
            taps.append(tree(a))
            a = [d[m] * a[m] for m in range(modes)]
        taps[0] = taps[0] + skip_v[pl.ds(g * SUB, SUB), :]

        def body(c, _):
            x = [xs[g, at(c * CHUNK + t), :] for t in range(CHUNK)]
            for t in range(CHUNK):
                base[g, at(c * CHUNK + t), :] = tree([taps[j] * x[t - j] for j in range(t + 1)])
            for m in range(modes):
                ends[g, at(c * modes + m), :] = mode(atm, g, m) * ends[g, at(c * modes + m), :]
            return 0

        lax.fori_loop(0, chunks, body, 0)

    def fix_edge(g):
        x0, x1 = edge[g, pl.ds(0, SUB), :], edge[g, pl.ds(SUB, SUB), :]
        sk = skip_v[pl.ds(g * SUB, SUB), :]
        lead = tree([mode(atm, g, m) * jnp.exp(mode(rtm, g, m)) for m in range(modes)])
        base[g, pl.ds(0, SUB), :] = sk * x0 - x1 * lead
        base[g, pl.ds(SUB, SUB), :] = sk * x1
        for m in range(modes):
            r = mode(rtm, g, m)
            ztm[g, pl.ds(m * SUB, SUB), :] = jnp.exp(r) * x0 + jnp.exp(2.0 * r) * x1

    split = (groups + 1) // 2
    for g in range(split):
        local(g)

    def add_outer(n, acc):
        remote(send2, recv2.at[n], s2_sem.at[0], r2_sem.at[n], dev(n * n1 + e)).wait_recv()
        return dec_out * acc + recv2[n].astype(F32)

    carried = lax.fori_loop(0, h, add_outer, jnp.zeros((modes, LANE), F32))
    for n in range(n1):
        send3[n] = (pre[n] + powr[n] * carried).astype(BF16)
    recv3[e] = send3[e]
    for n in ring_order():
        remote(send3.at[n], recv3.at[e], s3_sem.at[n], r3_sem.at[e], mate(n)).start()
    for g in range(split, groups):
        local(g)
    for g in range(groups):
        fix_edge(g)
    halo_q.wait_recv()
    for g in range(groups):
        h2, h1 = halo_of(0, g)
        t0, t1, t2 = tap(0, g)
        qtm[g, pl.ds(0, SUB), :] = qtm[g, pl.ds(0, SUB), :] + (t1 * h1 + t2 * h2)
        qtm[g, pl.ds(SUB, SUB), :] = qtm[g, pl.ds(SUB, SUB), :] + t2 * h1

    for g in range(groups):
        for s in range(SUB):
            n = g * SUB + s

            @pl.when(n != e)
            def _():
                remote(send3.at[n], recv3.at[n], s3_sem.at[n], r3_sem.at[n], mate(n)).wait_recv()

            ctm[g, pl.ds(s, modes, stride=SUB), :] = recv3[n].astype(F32)
        d = [mode(dtm, g, m) for m in range(modes)]
        init = tuple(mode(atm, g, m) * (mode(ctm, g, m) + mode(ztm, g, m)) for m in range(modes))

        def apply(c, buf, carry):
            s = list(carry)
            for t in range(CHUNK):
                s = [d[m] * s[m] for m in range(modes)]
                here = at(c * CHUNK + t)
                buf[pl.ds(t * SUB, SUB), :] = qtm[g, here, :] * (base[g, here, :] + tree(s))
            for w in range(SUB):
                v = buf[pl.ds(w, CHUNK, stride=SUB), :].astype(BF16)
                outb[pl.ds(pl.multiple_of(c * CHUNK, CHUNK), CHUNK), pl.ds(g * GROUP + w * LANE, LANE)] = v
            return tuple(s[m] + ends[g, at(c * modes + m), :] for m in range(modes))

        def applies(j, carry):
            return apply(2 * j + 1, ytmp2, apply(2 * j, ytmp, carry))

        lax.fori_loop(0, chunks // 2, applies, init)
        cols = pl.ds(g * GROUP, GROUP)
        pltpu.make_async_copy(outb.at[:, cols], out.at[:, cols], out_sem.at[g]).start()

    halo.wait_send()
    halo_q.wait_send()
    for n in range(n1):
        @pl.when(n != e)
        def _():
            for src, sem in ((send1, s1_sem), (send3, s3_sem)):
                remote(src.at[n], src.at[n], sem.at[n], sem.at[n], mate(n)).wait_send()
    for k in range(1, n2):
        @pl.when(h + k < n2)
        def _():
            remote(send2, send2, s2_sem.at[k], s2_sem.at[k], nxt).wait_send()
    for g in range(groups):
        cols = pl.ds(g * GROUP, GROUP)
        pltpu.make_async_copy(outb.at[:, cols], out.at[:, cols], out_sem.at[g]).wait()


def solution(mesh):
    outer_n, inner_n = mesh.shape["outer"], mesh.shape["inner"]

    def on_device(projected, short_taps, rates, residues, skip_gain):
        rows, width = projected.shape
        channels, modes = rates.shape
        groups = channels // GROUP
        n1 = channels // LANE
        n2 = outer_n * inner_n // n1
        any_spec = pl.BlockSpec(memory_space=pl.ANY)
        dma = pltpu.SemaphoreType.DMA
        tm = pltpu.VMEM((groups, rows * SUB, LANE), F32)
        pm = pltpu.VMEM((groups, modes * SUB, LANE), F32)
        tmp = pltpu.VMEM((CHUNK * SUB, LANE), F32)
        msg = pltpu.VMEM((n1, modes, LANE), BF16)
        return pl.pallas_call(
            functools.partial(kernel, (outer_n, inner_n, rows, channels, modes)),
            out_shape=jax.ShapeDtypeStruct((rows, channels), BF16),
            in_specs=[any_spec] * 5,
            out_specs=any_spec,
            scratch_shapes=[
                pltpu.VMEM((rows, width), BF16), tmp, tmp, tmp, tmp,
                pltpu.VMEM((3 * groups, CHUNK * SUB, LANE), F32), tm, tm, tm,
                pltpu.VMEM((3, width), F32), pltpu.VMEM((modes, channels), F32), pltpu.VMEM((modes, channels), F32),
                pltpu.VMEM((groups * SUB, LANE), F32), pltpu.VMEM((3 * 3 * groups * SUB, LANE), F32),
                pm, pm, pm, pm, pm,
                pltpu.VMEM((groups, rows // CHUNK * modes * SUB, LANE), F32),
                pltpu.VMEM((groups, 2 * SUB, LANE), F32), pltpu.VMEM((groups, 4 * SUB, LANE), F32),
                pltpu.VMEM((groups * SUB * modes, LANE), F32), pm,
                pltpu.VMEM((n1, modes, LANE), F32), pltpu.VMEM((n1, modes, LANE), F32),
                pltpu.VMEM((3 * groups, 2 * SUB, LANE), BF16), pltpu.VMEM((3 * groups, 2 * SUB, LANE), BF16),
                msg, msg, pltpu.VMEM((modes, LANE), BF16), pltpu.VMEM((n2, modes, LANE), BF16), msg, msg,
                tmp, tmp, pltpu.VMEM((rows, channels), BF16),
                dma((3 * groups + 2,)), dma((4,)), dma((groups,)), dma((2,)), dma((2,)),
                dma((n1,)), dma((n1,)), dma((n2,)), dma((n2,)), dma((n1,)), dma((n1,)),
            ],
            compiler_params=pltpu.CompilerParams(collective_id=0, has_side_effects=True,
                                                 vmem_limit_bytes=60 * 1024 * 1024),
            name="modal_scan",
        )(projected, short_taps, rates.T, residues.T, skip_gain.reshape(groups * SUB, LANE))

    return jax.shard_map(
        on_device, mesh=mesh,
        in_specs=(P(("outer", "inner"), None), P(), P(), P(), P()),
        out_specs=P(("outer", "inner"), None), check_vma=False,
    )
```

time: 39.6 us -> 35.6 us (0.90)
  the two profiles are of different devices: /device:TPU:20 before, /device:TPU:17 now
where the time goes in v3:
time: 35.6 us; the launch traced here: 35.2 us
  Pallas kernels  32.9 us (92%)
  local copies, waits for them, and re-layouts  2.29 us (6%)
    pallas_call x1, Pallas kernels, on_device(): pl.pallas_call(functools.partial(kernel, (outer_n, inner_n, rows, channel...  32.9 us
    unnamed x1, local copies, waits for them, and re-layouts  2.29 us

profile of v3, /device:TPU:17, one launch (start us, length us, event | category | flops | bytes accessed | tf_op | source)
XLA Modules:
  0.0 35.2 jit_solution(250446688278875968)
XLA Ops:
  0.0 32.9 %modal_scan.1 = bf16[128,4096]{1,0:T(8,128)(2,1)} custom-call(bf16[128,12288]{1,0:T(8,128)(2,1)} %proj.1, f32[3,12288]{1,0:T(4,128)} %taps_in.1, f32[16,4096]{1,0:T(8,128)} %bitcast.3, f32[16,4096]{1,0:T(8,128)} %bitcast.4, f32[32,128]{1,0:T(8,128)} %bitcast.5), custom_call_target="tpu_custom_call" | custom-call | tf_op jit(solution)/shard_map/modal_scan/pallas_call | solution.py:401
  32.9 2.3 %copy.7 = bf16[128,4096]{1,0:T(8,128)(2,1)} copy(bf16[128,4096]{1,0:T(8,128)(2,1)} %modal_scan.1) | data formatting | bytes 2097152

commit v4 on v3

--- a/solution.py
+++ b/solution.py
@@ -18,9 +18,9 @@
 
 
 def kernel(dims, proj, taps_in, rates_in, resid_in, skip_in, out, raw, ktmp, vtmp, ktmp2, vtmp2, ttmp, qtm, xs, base, taps_n,
-           rate_n, res_n, skip_v, taps_t, rtm, dtm, d16, atm, ztm, ends, edge, head, stg, ctm, pre, powr, hsend, hrecv,
-           send1, recv1, send2, recv2, send3, recv3, ytmp, ytmp2, outb, in_sem, par_sem, out_sem, hs_sem, hr_sem, s1_sem,
-           r1_sem, s2_sem, r2_sem, s3_sem, r3_sem):
+           rate_n, res_n, skip_v, taps_t, rtm, dtm, d16, atm, ztm, ends, edge, head, stg, ctm, pre, powr, hsend, hrecv, xstage, xwork, xwork2, xsend, xrecv,
+           send1, recv1, send2, recv2, send3, recv3, ytmp, ytmp2, in_sem, par_sem, hs_sem, hr_sem, xs_sem, xr_sem,
+           s1_sem, r1_sem, s2_sem, r2_sem, s3_sem, r3_sem):
     outer_n, inner_n, rows, channels, modes = dims
     groups = channels // GROUP
     chunks = rows // CHUNK
@@ -31,8 +31,29 @@
     p = lax.axis_index("outer") * inner_n + lax.axis_index("inner")
     e = lax.rem(p, n1)
     h = p // n1
-    far = lax.rem(p, RING) == RING - 1
-    near = lax.rem(p, RING) != 0
+    z = lax.rem(e, RING)
+    hi = e // RING
+    high = n1 // RING
+    zpg = RING // groups
+    near = z != 0
+    rim = jnp.logical_or(z == 0, z == RING - 1)
+    mine = (z // zpg) * SUB + hi * zpg + lax.rem(z, zpg)
+
+    def far_first(idx):
+        if groups == 1:
+            return 0
+        odd = lax.rem(z, 2)
+        off = (2, 1 + 2 * odd, 3 - 2 * odd, 0)
+        step = off[idx] if isinstance(idx, int) else jnp.where(
+            idx == 0, off[0], jnp.where(idx == 1, off[1], jnp.where(idx == 2, off[2], off[3])))
+        return lax.rem(z // zpg + step, groups)
+
+    def owner(n):
+        s = lax.rem(n, SUB) if not isinstance(n, int) else n % SUB
+        return (s // zpg) * RING + zpg * (n // SUB) + (s % zpg if isinstance(s, int) else lax.rem(s, zpg))
+
+    def own_by(g, s):
+        return (s // zpg) * RING + zpg * g + s % zpg
 
     def dev(r):
         return (r // inner_n, lax.rem(r, inner_n))
@@ -60,13 +81,13 @@
     par_cps[1].start()
 
     def in_copy(f, g):
-        cols = pl.ds((f * groups + g) * GROUP, GROUP)
+        cols = pl.ds(pl.multiple_of((f * groups + g) * GROUP, GROUP), GROUP)
         return pltpu.make_async_copy(proj.at[pl.ds(0, last), cols], raw.at[pl.ds(0, last), cols],
                                      in_sem.at[f * groups + g])
 
-    for g in range(groups):
-        in_copy(1, g).start()
-        in_copy(2, g).start()
+    for idx in range(groups):
+        in_copy(1, far_first(idx)).start()
+        in_copy(2, far_first(idx)).start()
     par_cps[2].start()
     par_cps[3].start()
     tails[1].start()
@@ -84,7 +105,7 @@
 
     def relay(dst, row, f, g, c):
         for s in range(SUB):
-            col = (f * groups + g) * GROUP + s * LANE
+            col = pl.multiple_of((f * groups + g) * GROUP + s * LANE, LANE)
             v = raw[pl.ds(pl.multiple_of(c * CHUNK, CHUNK), CHUNK), pl.ds(col, LANE)].astype(F32)
             dst[pl.ds(row + s, CHUNK, stride=SUB), :] = v
 
@@ -100,11 +121,39 @@
     halo = remote(hsend.at[kv_blocks], hrecv.at[kv_blocks], hs_sem.at[0], hr_sem.at[0], nxt)
     halo_q = remote(hsend.at[q_blocks], hrecv.at[q_blocks], hs_sem.at[1], hr_sem.at[1], nxt)
 
-    def send_halo():
-        pl.semaphore_wait(bar, n1 + n2)
-        halo.start()
-
-    pl.when(far)(send_halo)
+    def send_rim():
+        @pl.when(z == 0)
+        def _():
+            for g in range(groups):
+                for n, f in enumerate((1, 2)):
+                    relay(ktmp, 0, f, g, 0)
+                    xstage[g, pl.ds(n * 2 * SUB, 2 * SUB), :] = ktmp[pl.ds(0, 2 * SUB), :]
+
+        @pl.when(z != 0)
+        def _():
+            for g in range(groups):
+                for n, f in enumerate((1, 2)):
+                    xstage[g, pl.ds(n * 2 * SUB, 2 * SUB), :] = ttmp[f * groups + g, pl.ds((CHUNK - 2) * SUB, 2 * SUB), :]
+
+        for g in range(groups):
+            for t in range(SUB):
+                xsend[g * SUB + t] = xstage[g, pl.ds(t, 4, stride=SUB), :].astype(BF16)
+        slot = jnp.where(z == 0, hi, high + hi)
+
+        def one(n, _):
+            to = owner(n)
+
+            @pl.when(to == e)
+            def _():
+                xrecv[slot] = xsend[n]
+
+            @pl.when(to != e)
+            def _():
+                remote(xsend.at[n], xrecv.at[slot], xs_sem.at[n], xr_sem.at[slot], mate(to)).start()
+
+            return 0
+
+        lax.fori_loop(0, n1, one, 0)
 
     par_cps[0].wait()
     par_cps[1].wait()
@@ -121,7 +170,7 @@
         d16[g] = jnp.exp(-float(CHUNK) * r)
 
     def tap(f, g):
-        return [taps_t[pl.ds(((f * groups + g) * 3 + j) * SUB, SUB), :] for j in range(3)]
+        return [taps_t[pl.ds(pl.multiple_of(((f * groups + g) * 3 + j) * SUB, SUB), SUB), :] for j in range(3)]
 
     def mode(ref, g, m):
         return ref[g, pl.ds(m * SUB, SUB), :]
@@ -179,57 +228,65 @@
         both = jnp.where(first, jnp.zeros_like(both), both)
         return both[:SUB], both[SUB:]
 
-    def emit(g):
+    def edges(g):
         feats = []
         for n, f in enumerate((1, 2)):
             h2, h1 = halo_of(f, g)
             t0, t1, t2 = tap(f, g)
             e0, e1 = head[g, pl.ds(2 * n * SUB, SUB), :], head[g, pl.ds((2 * n + 1) * SUB, SUB), :]
             feats.append((t0 * e0 + t1 * h1 + t2 * h2, t0 * e1 + t1 * e0 + t2 * h1))
-        x0, x1 = feats[0][0] * feats[1][0], feats[0][1] * feats[1][1]
-        edge[g, pl.ds(0, SUB), :] = x0
-        edge[g, pl.ds(SUB, SUB), :] = x1
+        edge[g, pl.ds(0, SUB), :] = feats[0][0] * feats[1][0]
+        edge[g, pl.ds(SUB, SUB), :] = feats[0][1] * feats[1][1]
+
+    def emit(g):
+        @pl.when(near)
+        def _():
+            edges(g)
+
+        @pl.when(jnp.logical_not(near))
+        def _():
+            edge[g] = jnp.zeros((2 * SUB, LANE), F32)
+
+        x0, x1 = edge[g, pl.ds(0, SUB), :], edge[g, pl.ds(SUB, SUB), :]
         for m in range(modes):
             state = mode(ztm, g, m) + jnp.exp(-(rows - 2.0) * mode(rtm, g, m)) * (mode(dtm, g, m) * x0 + x1)
-            stg[pl.ds(g * SUB * modes + m, SUB, stride=modes), :] = state
+            stg[g, pl.ds(m, SUB, stride=modes), :] = state
         for s in range(SUB):
-            n = g * SUB + s
-            send1[n] = stg[pl.ds(n * modes, modes), :].astype(BF16)
+            send1[g * SUB + s] = stg[g, pl.ds(s * modes, modes), :].astype(BF16)
         for s in range(SUB):
-            n = g * SUB + s
-
-            @pl.when(n == e)
-            def _():
-                recv1[n] = send1[n]
-
-            @pl.when(n != e)
-            def _():
-                remote(send1.at[n], recv1.at[e], s1_sem.at[n], r1_sem.at[e], mate(n)).start()
+            n, to = g * SUB + s, own_by(g, s)
+
+            @pl.when(to == e)
+            def _():
+                recv1[e] = send1[n]
+
+            @pl.when(to != e)
+            def _():
+                remote(send1.at[n], recv1.at[e], s1_sem.at[n], r1_sem.at[e], mate(to)).start()
 
     early = groups - 1
-    for g in range(groups):
-        for f in (1, 2):
-            in_copy(f, g).wait()
-        states(g)
-        if g == (groups - 1) // 2:
-            pl.when(jnp.logical_not(far))(send_halo)
-        if g == early - 1:
+    for idx in range(groups):
+        if idx < 2:
+            for k in ((0,) if idx == 0 else range(1, groups)):
+                for f in (1, 2):
+                    in_copy(f, far_first(k)).wait()
+        states(far_first(idx))
+        if idx == (groups - 1) // 2:
+            pl.semaphore_wait(bar, n1 + n2)
+            halo.start()
+            pl.when(rim)(send_rim)
+        if idx == max(early - 1, 0):
             @pl.when(near)
             def _():
                 halo.wait_recv()
-                for n in range(early):
-                    emit(n)
-
-    def rest():
-        halo.wait_recv()
-        for n in range(early):
-            emit(n)
-
-    if early:
-        pl.when(jnp.logical_not(near))(rest)
-    else:
-        halo.wait_recv()
-    emit(groups - 1)
+
+            def emit_early(k, _):
+                emit(far_first(k))
+                return 0
+
+            if early:
+                lax.fori_loop(0, early, emit_early, 0)
+    emit(far_first(groups - 1))
 
     tails[1].wait()
     tail_of(0)
@@ -260,9 +317,35 @@
         relay(ktmp, 0, 0, g, 0)
         lax.fori_loop(0, chunks // 2, gates, (zero, zero))
 
-    own = rate_n[:, pl.ds(pl.multiple_of(e * LANE, LANE), LANE)]
+    own_cols = pl.ds(pl.multiple_of(mine * LANE, LANE), LANE)
+    own = rate_n[:, own_cols]
     dec_in = jnp.exp(-float(rows) * own)
     dec_out = jnp.exp(-float(rows * n1) * own)
+    dec_one, dec_edge = jnp.exp(-own), jnp.exp(-(rows - 2.0) * own)
+    own_taps = [taps_n[pl.ds(j, 1), pl.ds(pl.multiple_of(f * channels + mine * LANE, LANE), LANE)]
+                for f in (1, 2) for j in range(3)]
+
+    def rows_of(val):
+        xwork[...] = val
+        return [xwork[pl.ds(j, 1), :] for j in range(4)]
+
+    def edge_state(heads, tails):
+        ends_x = []
+        for j in (0, 1):
+            t0, t1, t2 = own_taps[3 * j:3 * j + 3]
+            e0, e1, h2, h1 = heads[2 * j], heads[2 * j + 1], tails[2 * j], tails[2 * j + 1]
+            ends_x.append((t0 * e0 + t1 * h1 + t2 * h2, t0 * e1 + t1 * e0 + t2 * h1))
+        x0, x1 = ends_x[0][0] * ends_x[1][0], ends_x[0][1] * ends_x[1][1]
+        return dec_edge * (dec_one * x0 + x1)
+
+    for k in range(high):
+        for slot, src in ((k, k * RING), (high + k, k * RING + RING - 1)):
+            @pl.when(src != e)
+            def _():
+                remote(xsend.at[0], xrecv.at[slot], xs_sem.at[0], xr_sem.at[slot], mate(src)).wait_recv()
+    fixes = [None] + [edge_state(rows_of(xrecv[k].astype(F32)), rows_of(xrecv[high + k - 1].astype(F32)))
+                      for k in range(1, high)]
+    send2[1, pl.ds(0, 8), :] = jnp.concatenate([xrecv[0].astype(F32), xrecv[2 * high - 1].astype(F32)], 0).astype(BF16)
     run = jnp.zeros((modes, LANE), F32)
     for n in range(n1):
         pre[n] = run
@@ -272,7 +355,9 @@
             remote(send1.at[n], recv1.at[n], s1_sem.at[n], r1_sem.at[n], mate(n)).wait_recv()
 
         run = dec_in * run + recv1[n].astype(F32)
-    send2[...] = run.astype(BF16)
+        if n % RING == 0 and n:
+            run = run + fixes[n // RING]
+    send2[0] = run.astype(BF16)
     for k in range(n2 - 1, 0, -1):
         @pl.when(h + k < n2)
         def _():
@@ -316,18 +401,34 @@
     for g in range(split):
         local(g)
 
-    def add_outer(n, acc):
+    def add_outer(n, carry):
+        acc, tails = carry[0], carry[1:]
         remote(send2, recv2.at[n], s2_sem.at[0], r2_sem.at[n], dev(n * n1 + e)).wait_recv()
-        return dec_out * acc + recv2[n].astype(F32)
-
-    carried = lax.fori_loop(0, h, add_outer, jnp.zeros((modes, LANE), F32))
-    for n in range(n1):
-        send3[n] = (pre[n] + powr[n] * carried).astype(BF16)
-    recv3[e] = send3[e]
+        xwork2[...] = recv2[n, 1, pl.ds(0, 8), :].astype(F32)
+        both = [xwork2[pl.ds(j, 1), :] for j in range(8)]
+        whole = recv2[n, 0].astype(F32) + last_power * edge_state(both[:4], tails)
+        return (dec_out * acc + whole, *both[4:])
+
+    last_power = powr[n1 - 1]
+    none = jnp.zeros((1, LANE), F32)
+    done = lax.fori_loop(0, h, add_outer, (jnp.zeros((modes, LANE), F32), none, none, none, none))
+    carried = done[0]
+    after = dec_in * carried + edge_state(rows_of(xrecv[0].astype(F32)), done[1:])
+    send3[0] = carried.astype(BF16)
+    for n in range(1, n1):
+        send3[n] = (pre[n] + powr[n - 1] * after).astype(BF16)
+    recv3[mine] = send3[e]
     for n in ring_order():
-        remote(send3.at[n], recv3.at[e], s3_sem.at[n], r3_sem.at[e], mate(n)).start()
+        remote(send3.at[n], recv3.at[mine], s3_sem.at[n], r3_sem.at[mine], mate(n)).start()
     for g in range(split, groups):
         local(g)
+
+    @pl.when(jnp.logical_not(near))
+    def _():
+        halo.wait_recv()
+        for g in range(groups):
+            edges(g)
+
     for g in range(groups):
         fix_edge(g)
     halo_q.wait_recv()
@@ -337,13 +438,14 @@
         qtm[g, pl.ds(0, SUB), :] = qtm[g, pl.ds(0, SUB), :] + (t1 * h1 + t2 * h2)
         qtm[g, pl.ds(SUB, SUB), :] = qtm[g, pl.ds(SUB, SUB), :] + t2 * h1
 
-    for g in range(groups):
+    for idx in range(groups - 1, -1, -1):
+        g = far_first(idx)
         for s in range(SUB):
-            n = g * SUB + s
-
-            @pl.when(n != e)
-            def _():
-                remote(send3.at[n], recv3.at[n], s3_sem.at[n], r3_sem.at[n], mate(n)).wait_recv()
+            n, src = g * SUB + s, own_by(g, s)
+
+            @pl.when(src != e)
+            def _():
+                remote(send3.at[n], recv3.at[n], s3_sem.at[n], r3_sem.at[n], mate(src)).wait_recv()
 
             ctm[g, pl.ds(s, modes, stride=SUB), :] = recv3[n].astype(F32)
         d = [mode(dtm, g, m) for m in range(modes)]
@@ -357,30 +459,38 @@
                 buf[pl.ds(t * SUB, SUB), :] = qtm[g, here, :] * (base[g, here, :] + tree(s))
             for w in range(SUB):
                 v = buf[pl.ds(w, CHUNK, stride=SUB), :].astype(BF16)
-                outb[pl.ds(pl.multiple_of(c * CHUNK, CHUNK), CHUNK), pl.ds(g * GROUP + w * LANE, LANE)] = v
+                cols = pl.ds(pl.multiple_of(g * GROUP + w * LANE, LANE), LANE)
+                out[pl.ds(pl.multiple_of(c * CHUNK, CHUNK), CHUNK), cols] = v
             return tuple(s[m] + ends[g, at(c * modes + m), :] for m in range(modes))
 
         def applies(j, carry):
             return apply(2 * j + 1, ytmp2, apply(2 * j, ytmp, carry))
 
         lax.fori_loop(0, chunks // 2, applies, init)
-        cols = pl.ds(g * GROUP, GROUP)
-        pltpu.make_async_copy(outb.at[:, cols], out.at[:, cols], out_sem.at[g]).start()
 
     halo.wait_send()
     halo_q.wait_send()
-    for n in range(n1):
+
+    def drain(n, _):
+        @pl.when(n != mine)
+        def _():
+            remote(send1.at[n], send1.at[n], s1_sem.at[n], s1_sem.at[n], nxt).wait_send()
+
         @pl.when(n != e)
         def _():
-            for src, sem in ((send1, s1_sem), (send3, s3_sem)):
-                remote(src.at[n], src.at[n], sem.at[n], sem.at[n], mate(n)).wait_send()
+            remote(send3.at[n], send3.at[n], s3_sem.at[n], s3_sem.at[n], nxt).wait_send()
+
+        @pl.when(jnp.logical_and(rim, n != mine))
+        def _():
+            remote(xsend.at[n], xsend.at[n], xs_sem.at[n], xs_sem.at[n], nxt).wait_send()
+
+        return 0
+
+    lax.fori_loop(0, n1, drain, 0)
     for k in range(1, n2):
         @pl.when(h + k < n2)
         def _():
             remote(send2, send2, s2_sem.at[k], s2_sem.at[k], nxt).wait_send()
-    for g in range(groups):
-        cols = pl.ds(g * GROUP, GROUP)
-        pltpu.make_async_copy(outb.at[:, cols], out.at[:, cols], out_sem.at[g]).wait()
 
 
 def solution(mesh):
@@ -400,9 +510,9 @@
         msg = pltpu.VMEM((n1, modes, LANE), BF16)
         return pl.pallas_call(
             functools.partial(kernel, (outer_n, inner_n, rows, channels, modes)),
-            out_shape=jax.ShapeDtypeStruct((rows, channels), BF16),
+            out_shape=pltpu.VMEM((rows, channels), BF16),
             in_specs=[any_spec] * 5,
-            out_specs=any_spec,
+            out_specs=pl.BlockSpec(memory_space=pltpu.VMEM),
             scratch_shapes=[
                 pltpu.VMEM((rows, width), BF16), tmp, tmp, tmp, tmp,
                 pltpu.VMEM((3 * groups, CHUNK * SUB, LANE), F32), tm, tm, tm,
@@ -411,12 +521,14 @@
                 pm, pm, pm, pm, pm,
                 pltpu.VMEM((groups, rows // CHUNK * modes * SUB, LANE), F32),
                 pltpu.VMEM((groups, 2 * SUB, LANE), F32), pltpu.VMEM((groups, 4 * SUB, LANE), F32),
-                pltpu.VMEM((groups * SUB * modes, LANE), F32), pm,
+                pm, pm,
                 pltpu.VMEM((n1, modes, LANE), F32), pltpu.VMEM((n1, modes, LANE), F32),
                 pltpu.VMEM((3 * groups, 2 * SUB, LANE), BF16), pltpu.VMEM((3 * groups, 2 * SUB, LANE), BF16),
-                msg, msg, pltpu.VMEM((modes, LANE), BF16), pltpu.VMEM((n2, modes, LANE), BF16), msg, msg,
-                tmp, tmp, pltpu.VMEM((rows, channels), BF16),
-                dma((3 * groups + 2,)), dma((4,)), dma((groups,)), dma((2,)), dma((2,)),
+                pltpu.VMEM((groups, 4 * SUB, LANE), F32), pltpu.VMEM((4, LANE), F32), pltpu.VMEM((8, LANE), F32),
+                pltpu.VMEM((n1, 4, LANE), BF16), pltpu.VMEM((2 * n1 // RING, 4, LANE), BF16),
+                msg, msg, pltpu.VMEM((2, modes, LANE), BF16), pltpu.VMEM((n2, 2, modes, LANE), BF16), msg, msg,
+                tmp, tmp,
+                dma((3 * groups + 2,)), dma((4,)), dma((2,)), dma((2,)), dma((n1,)), dma((2 * n1 // RING,)),
                 dma((n1,)), dma((n1,)), dma((n2,)), dma((n2,)), dma((n1,)), dma((n1,)),
             ],
             compiler_params=pltpu.CompilerParams(collective_id=0, has_side_effects=True,

time: 35.6 us -> 33.3 us (0.935)
  local copies, waits for them, and re-layouts: 2.29 us -> 0.97 us
  Pallas kernels: 32.9 us -> 32.3 us
    unnamed x1, local copies, waits for them, and re-layouts: 2.29 us -> 0.97 us
    pallas_call x1, Pallas kernels: 32.9 us -> 32.3 us  [on_device(): pl.pallas_call(functools.partial(kernel, (outer_n, inner_n, rows, channel...]
where the time goes in v4:
time: 33.3 us; the launch traced here: 33.2 us
  Pallas kernels  32.3 us (97%)
  local copies, waits for them, and re-layouts  0.97 us (3%)
    pallas_call x1, Pallas kernels, on_device(): pl.pallas_call(functools.partial(kernel, (outer_n, inner_n, rows, channel...  32.3 us
    unnamed x1, local copies, waits for them, and re-layouts  0.97 us

profile of v4, /device:TPU:17, one launch (start us, length us, event | category | flops | bytes accessed | tf_op | source)
XLA Modules:
  0.0 33.2 jit_solution(14694850044037731195)
XLA Ops:
  0.0 32.3 %modal_scan.1 = bf16[128,4096]{1,0:T(8,128)(2,1)S(1)} custom-call(bf16[128,12288]{1,0:T(8,128)(2,1)} %proj.1, f32[3,12288]{1,0:T(4,128)} %taps_in.1, f32[16,4096]{1,0:T(8,128)} %bitcast.3, f32[16,4096]{1,0:T(8,128)} %bitcast.4, f32[32,128]{1,0:T(8,128)} %bitcast.5), custom_call_target="tpu_custom_call" | custom-call | tf_op jit(solution)/shard_map/modal_scan/pallas_call | solution.py:511
  32.3 1.0 %copy.7 = bf16[128,4096]{1,0:T(8,128)(2,1)} copy(bf16[128,4096]{1,0:T(8,128)(2,1)S(1)} %modal_scan.1) | data formatting | bytes 2097152

commit v5 on v4

--- a/solution.py
+++ b/solution.py
@@ -18,8 +18,8 @@
 
 
 def kernel(dims, proj, taps_in, rates_in, resid_in, skip_in, out, raw, ktmp, vtmp, ktmp2, vtmp2, ttmp, qtm, xs, base, taps_n,
-           rate_n, res_n, skip_v, taps_t, rtm, dtm, d16, atm, ztm, ends, edge, head, stg, ctm, pre, powr, hsend, hrecv, xstage, xwork, xwork2, xsend, xrecv,
-           send1, recv1, send2, recv2, send3, recv3, ytmp, ytmp2, in_sem, par_sem, hs_sem, hr_sem, xs_sem, xr_sem,
+           rate_n, res_n, skip_v, taps_t, rtm, dtm, d16, atm, ztm, ends, edge, head, stg, ctm, pre, powr, hsend, hrecv, xwork,
+           send1, recv1, send2, recv2, send3, recv3, ytmp, ytmp2, in_sem, par_sem, hs_sem, hr_sem,
            s1_sem, r1_sem, s2_sem, r2_sem, s3_sem, r3_sem):
     outer_n, inner_n, rows, channels, modes = dims
     groups = channels // GROUP
@@ -33,10 +33,8 @@
     h = p // n1
     z = lax.rem(e, RING)
     hi = e // RING
-    high = n1 // RING
     zpg = RING // groups
-    near = z != 0
-    rim = jnp.logical_or(z == 0, z == RING - 1)
+    late = z >= RING // 2
     mine = (z // zpg) * SUB + hi * zpg + lax.rem(z, zpg)
 
     def far_first(idx):
@@ -48,10 +46,6 @@
             idx == 0, off[0], jnp.where(idx == 1, off[1], jnp.where(idx == 2, off[2], off[3])))
         return lax.rem(z // zpg + step, groups)
 
-    def owner(n):
-        s = lax.rem(n, SUB) if not isinstance(n, int) else n % SUB
-        return (s // zpg) * RING + zpg * (n // SUB) + (s % zpg if isinstance(s, int) else lax.rem(s, zpg))
-
     def own_by(g, s):
         return (s // zpg) * RING + zpg * g + s % zpg
 
@@ -111,49 +105,16 @@
 
     def tail_of(f):
         for g in range(groups):
-            relay(ttmp.at[f * groups + g], 0, f, g, chunks - 1)
-            hsend[f * groups + g] = ttmp[f * groups + g, pl.ds((CHUNK - 2) * SUB, 2 * SUB), :].astype(BF16)
+            relay(ttmp.at[g], 0, f, g, chunks - 1)
+            tail = ttmp[g, pl.ds((CHUNK - 2) * SUB, 2 * SUB), :]
+            hsend[f * groups + g] = tail.astype(BF16)
+            if f:
+                head[g, pl.ds((2 + 2 * f) * SUB, 2 * SUB), :] = tail
 
     tails[0].wait()
     tail_of(1)
     tail_of(2)
-    kv_blocks, q_blocks = pl.ds(groups, 2 * groups), pl.ds(0, groups)
-    halo = remote(hsend.at[kv_blocks], hrecv.at[kv_blocks], hs_sem.at[0], hr_sem.at[0], nxt)
-    halo_q = remote(hsend.at[q_blocks], hrecv.at[q_blocks], hs_sem.at[1], hr_sem.at[1], nxt)
-
-    def send_rim():
-        @pl.when(z == 0)
-        def _():
-            for g in range(groups):
-                for n, f in enumerate((1, 2)):
-                    relay(ktmp, 0, f, g, 0)
-                    xstage[g, pl.ds(n * 2 * SUB, 2 * SUB), :] = ktmp[pl.ds(0, 2 * SUB), :]
-
-        @pl.when(z != 0)
-        def _():
-            for g in range(groups):
-                for n, f in enumerate((1, 2)):
-                    xstage[g, pl.ds(n * 2 * SUB, 2 * SUB), :] = ttmp[f * groups + g, pl.ds((CHUNK - 2) * SUB, 2 * SUB), :]
-
-        for g in range(groups):
-            for t in range(SUB):
-                xsend[g * SUB + t] = xstage[g, pl.ds(t, 4, stride=SUB), :].astype(BF16)
-        slot = jnp.where(z == 0, hi, high + hi)
-
-        def one(n, _):
-            to = owner(n)
-
-            @pl.when(to == e)
-            def _():
-                xrecv[slot] = xsend[n]
-
-            @pl.when(to != e)
-            def _():
-                remote(xsend.at[n], xrecv.at[slot], xs_sem.at[n], xr_sem.at[slot], mate(to)).start()
-
-            return 0
-
-        lax.fori_loop(0, n1, one, 0)
+    halo = remote(hsend, hrecv, hs_sem, hr_sem, nxt)
 
     par_cps[0].wait()
     par_cps[1].wait()
@@ -239,20 +200,11 @@
         edge[g, pl.ds(SUB, SUB), :] = feats[0][1] * feats[1][1]
 
     def emit(g):
-        @pl.when(near)
-        def _():
-            edges(g)
-
-        @pl.when(jnp.logical_not(near))
-        def _():
-            edge[g] = jnp.zeros((2 * SUB, LANE), F32)
-
-        x0, x1 = edge[g, pl.ds(0, SUB), :], edge[g, pl.ds(SUB, SUB), :]
         for m in range(modes):
-            state = mode(ztm, g, m) + jnp.exp(-(rows - 2.0) * mode(rtm, g, m)) * (mode(dtm, g, m) * x0 + x1)
-            stg[g, pl.ds(m, SUB, stride=modes), :] = state
-        for s in range(SUB):
-            send1[g * SUB + s] = stg[g, pl.ds(s * modes, modes), :].astype(BF16)
+            stg[g, pl.ds(m, SUB, stride=modes), :] = mode(ztm, g, m)
+        for s in range(SUB):
+            send1[g * SUB + s, pl.ds(0, modes), :] = stg[g, pl.ds(s * modes, modes), :].astype(BF16)
+            send1[g * SUB + s, pl.ds(modes, SUB), :] = head[g, pl.ds(s, SUB, stride=SUB), :].astype(BF16)
         for s in range(SUB):
             n, to = g * SUB + s, own_by(g, s)
 
@@ -264,33 +216,39 @@
             def _():
                 remote(send1.at[n], recv1.at[e], s1_sem.at[n], r1_sem.at[e], mate(to)).start()
 
-    early = groups - 1
+    def emit_all(k, _):
+        emit(far_first(k))
+        return 0
+
+    half = min(2, groups - 1)
     for idx in range(groups):
         if idx < 2:
             for k in ((0,) if idx == 0 else range(1, groups)):
                 for f in (1, 2):
                     in_copy(f, far_first(k)).wait()
         states(far_first(idx))
-        if idx == (groups - 1) // 2:
+        if idx == half - 1:
+            @pl.when(late)
+            def _():
+                pl.semaphore_wait(bar, n1 + n2)
+                lax.fori_loop(0, half, emit_all, 0)
+        elif half <= idx < groups - 1:
+            @pl.when(late)
+            def _():
+                emit(far_first(idx))
+
+    if half:
+        @pl.when(jnp.logical_not(late))
+        def _():
             pl.semaphore_wait(bar, n1 + n2)
-            halo.start()
-            pl.when(rim)(send_rim)
-        if idx == max(early - 1, 0):
-            @pl.when(near)
-            def _():
-                halo.wait_recv()
-
-            def emit_early(k, _):
-                emit(far_first(k))
-                return 0
-
-            if early:
-                lax.fori_loop(0, early, emit_early, 0)
+            lax.fori_loop(0, groups - 1, emit_all, 0)
+    else:
+        pl.semaphore_wait(bar, n1 + n2)
     emit(far_first(groups - 1))
 
     tails[1].wait()
     tail_of(0)
-    halo_q.start()
+    halo.start()
     par_cps[2].wait()
     par_cps[3].wait()
     for g in range(groups):
@@ -325,9 +283,8 @@
     own_taps = [taps_n[pl.ds(j, 1), pl.ds(pl.multiple_of(f * channels + mine * LANE, LANE), LANE)]
                 for f in (1, 2) for j in range(3)]
 
-    def rows_of(val):
-        xwork[...] = val
-        return [xwork[pl.ds(j, 1), :] for j in range(4)]
+    def row(base_row, j):
+        return xwork[pl.ds(base_row + j, 1), :]
 
     def edge_state(heads, tails):
         ends_x = []
@@ -338,14 +295,6 @@
         x0, x1 = ends_x[0][0] * ends_x[1][0], ends_x[0][1] * ends_x[1][1]
         return dec_edge * (dec_one * x0 + x1)
 
-    for k in range(high):
-        for slot, src in ((k, k * RING), (high + k, k * RING + RING - 1)):
-            @pl.when(src != e)
-            def _():
-                remote(xsend.at[0], xrecv.at[slot], xs_sem.at[0], xr_sem.at[slot], mate(src)).wait_recv()
-    fixes = [None] + [edge_state(rows_of(xrecv[k].astype(F32)), rows_of(xrecv[high + k - 1].astype(F32)))
-                      for k in range(1, high)]
-    send2[1, pl.ds(0, 8), :] = jnp.concatenate([xrecv[0].astype(F32), xrecv[2 * high - 1].astype(F32)], 0).astype(BF16)
     run = jnp.zeros((modes, LANE), F32)
     for n in range(n1):
         pre[n] = run
@@ -354,9 +303,12 @@
         def _():
             remote(send1.at[n], recv1.at[n], s1_sem.at[n], r1_sem.at[n], mate(n)).wait_recv()
 
-        run = dec_in * run + recv1[n].astype(F32)
-        if n % RING == 0 and n:
-            run = run + fixes[n // RING]
+        run = dec_in * run + recv1[n, pl.ds(0, modes), :].astype(F32)
+        xwork[pl.ds(n * SUB, SUB), :] = recv1[n, pl.ds(modes, SUB), :].astype(F32)
+        if n:
+            run = run + edge_state([row(n * SUB, j) for j in range(4)], [row((n - 1) * SUB + 4, j) for j in range(4)])
+    rim = [xwork[pl.ds(0, 4), :], xwork[pl.ds((n1 - 1) * SUB + 4, 4), :]]
+    send2[1, pl.ds(0, 8), :] = jnp.concatenate(rim, 0).astype(BF16)
     send2[0] = run.astype(BF16)
     for k in range(n2 - 1, 0, -1):
         @pl.when(h + k < n2)
@@ -404,8 +356,8 @@
     def add_outer(n, carry):
         acc, tails = carry[0], carry[1:]
         remote(send2, recv2.at[n], s2_sem.at[0], r2_sem.at[n], dev(n * n1 + e)).wait_recv()
-        xwork2[...] = recv2[n, 1, pl.ds(0, 8), :].astype(F32)
-        both = [xwork2[pl.ds(j, 1), :] for j in range(8)]
+        xwork[pl.ds(n1 * SUB, SUB), :] = recv2[n, 1, pl.ds(0, 8), :].astype(F32)
+        both = [row(n1 * SUB, j) for j in range(8)]
         whole = recv2[n, 0].astype(F32) + last_power * edge_state(both[:4], tails)
         return (dec_out * acc + whole, *both[4:])
 
@@ -413,7 +365,7 @@
     none = jnp.zeros((1, LANE), F32)
     done = lax.fori_loop(0, h, add_outer, (jnp.zeros((modes, LANE), F32), none, none, none, none))
     carried = done[0]
-    after = dec_in * carried + edge_state(rows_of(xrecv[0].astype(F32)), done[1:])
+    after = dec_in * carried + edge_state([row(0, j) for j in range(4)], done[1:])
     send3[0] = carried.astype(BF16)
     for n in range(1, n1):
         send3[n] = (pre[n] + powr[n - 1] * after).astype(BF16)
@@ -422,16 +374,10 @@
         remote(send3.at[n], recv3.at[mine], s3_sem.at[n], r3_sem.at[mine], mate(n)).start()
     for g in range(split, groups):
         local(g)
-
-    @pl.when(jnp.logical_not(near))
-    def _():
-        halo.wait_recv()
-        for g in range(groups):
-            edges(g)
-
-    for g in range(groups):
+    halo.wait_recv()
+    for g in range(groups):
+        edges(g)
         fix_edge(g)
-    halo_q.wait_recv()
     for g in range(groups):
         h2, h1 = halo_of(0, g)
         t0, t1, t2 = tap(0, g)
@@ -469,7 +415,6 @@
         lax.fori_loop(0, chunks // 2, applies, init)
 
     halo.wait_send()
-    halo_q.wait_send()
 
     def drain(n, _):
         @pl.when(n != mine)
@@ -479,10 +424,6 @@
         @pl.when(n != e)
         def _():
             remote(send3.at[n], send3.at[n], s3_sem.at[n], s3_sem.at[n], nxt).wait_send()
-
-        @pl.when(jnp.logical_and(rim, n != mine))
-        def _():
-            remote(xsend.at[n], xsend.at[n], xs_sem.at[n], xs_sem.at[n], nxt).wait_send()
 
         return 0
 
@@ -508,6 +449,7 @@
         pm = pltpu.VMEM((groups, modes * SUB, LANE), F32)
         tmp = pltpu.VMEM((CHUNK * SUB, LANE), F32)
         msg = pltpu.VMEM((n1, modes, LANE), BF16)
+        first_msg = pltpu.VMEM((n1, modes + SUB, LANE), BF16)
         return pl.pallas_call(
             functools.partial(kernel, (outer_n, inner_n, rows, channels, modes)),
             out_shape=pltpu.VMEM((rows, channels), BF16),
@@ -515,20 +457,19 @@
             out_specs=pl.BlockSpec(memory_space=pltpu.VMEM),
             scratch_shapes=[
                 pltpu.VMEM((rows, width), BF16), tmp, tmp, tmp, tmp,
-                pltpu.VMEM((3 * groups, CHUNK * SUB, LANE), F32), tm, tm, tm,
+                pltpu.VMEM((groups, CHUNK * SUB, LANE), F32), tm, tm, tm,
                 pltpu.VMEM((3, width), F32), pltpu.VMEM((modes, channels), F32), pltpu.VMEM((modes, channels), F32),
                 pltpu.VMEM((groups * SUB, LANE), F32), pltpu.VMEM((3 * 3 * groups * SUB, LANE), F32),
                 pm, pm, pm, pm, pm,
                 pltpu.VMEM((groups, rows // CHUNK * modes * SUB, LANE), F32),
-                pltpu.VMEM((groups, 2 * SUB, LANE), F32), pltpu.VMEM((groups, 4 * SUB, LANE), F32),
+                pltpu.VMEM((groups, 2 * SUB, LANE), F32), pltpu.VMEM((groups, 8 * SUB, LANE), F32),
                 pm, pm,
                 pltpu.VMEM((n1, modes, LANE), F32), pltpu.VMEM((n1, modes, LANE), F32),
                 pltpu.VMEM((3 * groups, 2 * SUB, LANE), BF16), pltpu.VMEM((3 * groups, 2 * SUB, LANE), BF16),
-                pltpu.VMEM((groups, 4 * SUB, LANE), F32), pltpu.VMEM((4, LANE), F32), pltpu.VMEM((8, LANE), F32),
-                pltpu.VMEM((n1, 4, LANE), BF16), pltpu.VMEM((2 * n1 // RING, 4, LANE), BF16),
-                msg, msg, pltpu.VMEM((2, modes, LANE), BF16), pltpu.VMEM((n2, 2, modes, LANE), BF16), msg, msg,
+                pltpu.VMEM(((n1 + 1) * SUB, LANE), F32), first_msg, first_msg,
+                pltpu.VMEM((2, modes, LANE), BF16), pltpu.VMEM((n2, 2, modes, LANE), BF16), msg, msg,
                 tmp, tmp,
-                dma((3 * groups + 2,)), dma((4,)), dma((2,)), dma((2,)), dma((n1,)), dma((2 * n1 // RING,)),
+                dma((3 * groups + 2,)), dma((4,)), dma, dma,
                 dma((n1,)), dma((n1,)), dma((n2,)), dma((n2,)), dma((n1,)), dma((n1,)),
             ],
             compiler_params=pltpu.CompilerParams(collective_id=0, has_side_effects=True,

time: 33.3 us -> 31.8 us (0.955)
  Pallas kernels: 32.3 us -> 30.7 us
    pallas_call x1, Pallas kernels: 32.3 us -> 30.7 us  [on_device(): pl.pallas_call(functools.partial(kernel, (outer_n, inner_n, rows, channel...]
where the time goes in v5:
time: 31.8 us; the launch traced here: 31.7 us
  Pallas kernels  30.7 us (97%)
  local copies, waits for them, and re-layouts  0.97 us (3%)
    pallas_call x1, Pallas kernels, on_device(): pl.pallas_call(functools.partial(kernel, (outer_n, inner_n, rows, channel...  30.7 us
    unnamed x1, local copies, waits for them, and re-layouts  0.97 us

profile of v5, /device:TPU:17, one launch (start us, length us, event | category | flops | bytes accessed | tf_op | source)
XLA Modules:
  0.0 31.7 jit_solution(2978380879376631512)
XLA Ops:
  0.0 30.7 %modal_scan.1 = bf16[128,4096]{1,0:T(8,128)(2,1)S(1)} custom-call(bf16[128,12288]{1,0:T(8,128)(2,1)} %proj.1, f32[3,12288]{1,0:T(4,128)} %taps_in.1, f32[16,4096]{1,0:T(8,128)} %bitcast.3, f32[16,4096]{1,0:T(8,128)} %bitcast.4, f32[32,128]{1,0:T(8,128)} %bitcast.5), custom_call_target="tpu_custom_call" | custom-call | tf_op jit(solution)/shard_map/modal_scan/pallas_call | solution.py:453
  30.8 1.0 %copy.7 = bf16[128,4096]{1,0:T(8,128)(2,1)} copy(bf16[128,4096]{1,0:T(8,128)(2,1)S(1)} %modal_scan.1) | data formatting | bytes 2097152

commit v6 on v5

--- a/solution.py
+++ b/solution.py
@@ -65,6 +65,15 @@
         return pltpu.make_async_remote_copy(src_ref=src, dst_ref=dst, send_sem=ssem, recv_sem=rsem, device_id=to,
                                             device_id_type=MESH)
 
+    bar = pltpu.get_barrier_semaphore()
+    nxt, prv = dev(lax.rem(p + 1, total)), dev(lax.rem(p + total - 1, total))
+    for n in ring_order():
+        pl.semaphore_signal(bar, inc=1, device_id=mate(n), device_id_type=MESH)
+    for to in (nxt, prv):
+        pl.semaphore_signal(bar, inc=1, device_id=to, device_id_type=MESH)
+    for k in range(1, n2):
+        pl.semaphore_signal(bar, inc=1, device_id=dev(lax.rem(h + k, n2) * n1 + e), device_id_type=MESH)
+
     kv = pl.ds(channels, 2 * channels)
     tails = [pltpu.make_async_copy(proj.at[pl.ds(last, CHUNK), c], raw.at[pl.ds(last, CHUNK), c], in_sem.at[3 * groups + n])
              for n, c in enumerate((kv, pl.ds(0, channels)))]
@@ -87,15 +96,6 @@
     tails[1].start()
     for g in range(groups):
         in_copy(0, g).start()
-
-    bar = pltpu.get_barrier_semaphore()
-    nxt, prv = dev(lax.rem(p + 1, total)), dev(lax.rem(p + total - 1, total))
-    for to in (nxt, prv):
-        pl.semaphore_signal(bar, inc=1, device_id=to, device_id_type=MESH)
-    for k in range(1, n2):
-        pl.semaphore_signal(bar, inc=1, device_id=dev(lax.rem(h + k, n2) * n1 + e), device_id_type=MESH)
-    for n in ring_order():
-        pl.semaphore_signal(bar, inc=1, device_id=mate(n), device_id_type=MESH)
 
     def relay(dst, row, f, g, c):
         for s in range(SUB):
@@ -199,12 +199,14 @@
         edge[g, pl.ds(0, SUB), :] = feats[0][0] * feats[1][0]
         edge[g, pl.ds(SUB, SUB), :] = feats[0][1] * feats[1][1]
 
-    def emit(g):
+    def stage(g):
         for m in range(modes):
             stg[g, pl.ds(m, SUB, stride=modes), :] = mode(ztm, g, m)
         for s in range(SUB):
             send1[g * SUB + s, pl.ds(0, modes), :] = stg[g, pl.ds(s * modes, modes), :].astype(BF16)
             send1[g * SUB + s, pl.ds(modes, SUB), :] = head[g, pl.ds(s, SUB, stride=SUB), :].astype(BF16)
+
+    def emit(g):
         for s in range(SUB):
             n, to = g * SUB + s, own_by(g, s)
 
@@ -227,6 +229,7 @@
                 for f in (1, 2):
                     in_copy(f, far_first(k)).wait()
         states(far_first(idx))
+        stage(far_first(idx))
         if idx == half - 1:
             @pl.when(late)
             def _():
@@ -370,7 +373,7 @@
     for n in range(1, n1):
         send3[n] = (pre[n] + powr[n - 1] * after).astype(BF16)
     recv3[mine] = send3[e]
-    for n in ring_order():
+    for n in list(ring_order())[::-1]:
         remote(send3.at[n], recv3.at[mine], s3_sem.at[n], r3_sem.at[mine], mate(n)).start()
     for g in range(split, groups):
         local(g)
@@ -383,6 +386,26 @@
         t0, t1, t2 = tap(0, g)
         qtm[g, pl.ds(0, SUB), :] = qtm[g, pl.ds(0, SUB), :] + (t1 * h1 + t2 * h2)
         qtm[g, pl.ds(SUB, SUB), :] = qtm[g, pl.ds(SUB, SUB), :] + t2 * h1
+
+    def drained():
+        halo.wait_send()
+
+        def drain(n, _):
+            @pl.when(n != mine)
+            def _():
+                remote(send1.at[n], send1.at[n], s1_sem.at[n], s1_sem.at[n], nxt).wait_send()
+
+            @pl.when(n != e)
+            def _():
+                remote(send3.at[n], send3.at[n], s3_sem.at[n], s3_sem.at[n], nxt).wait_send()
+
+            return 0
+
+        lax.fori_loop(0, n1, drain, 0)
+        for k in range(1, n2):
+            @pl.when(h + k < n2)
+            def _():
+                remote(send2, send2, s2_sem.at[k], s2_sem.at[k], nxt).wait_send()
 
     for idx in range(groups - 1, -1, -1):
         g = far_first(idx)
@@ -413,25 +436,8 @@
             return apply(2 * j + 1, ytmp2, apply(2 * j, ytmp, carry))
 
         lax.fori_loop(0, chunks // 2, applies, init)
-
-    halo.wait_send()
-
-    def drain(n, _):
-        @pl.when(n != mine)
-        def _():
-            remote(send1.at[n], send1.at[n], s1_sem.at[n], s1_sem.at[n], nxt).wait_send()
-
-        @pl.when(n != e)
-        def _():
-            remote(send3.at[n], send3.at[n], s3_sem.at[n], s3_sem.at[n], nxt).wait_send()
-
-        return 0
-
-    lax.fori_loop(0, n1, drain, 0)
-    for k in range(1, n2):
-        @pl.when(h + k < n2)
-        def _():
-            remote(send2, send2, s2_sem.at[k], s2_sem.at[k], nxt).wait_send()
+        if idx == min(1, groups - 1):
+            drained()
 
 
 def solution(mesh):

time: 31.8 us -> 31.1 us (0.978)
  Pallas kernels: 30.7 us -> 30.1 us
    pallas_call x1, Pallas kernels: 30.7 us -> 30.1 us  [on_device(): pl.pallas_call(functools.partial(kernel, (outer_n, inner_n, rows, channel...]
where the time goes in v6:
time: 31.1 us
  Pallas kernels  30.1 us (97%)
  local copies, waits for them, and re-layouts  0.97 us (3%)
    pallas_call x1, Pallas kernels, on_device(): pl.pallas_call(functools.partial(kernel, (outer_n, inner_n, rows, channel...  30.1 us
    unnamed x1, local copies, waits for them, and re-layouts  0.97 us

profile of v6, /device:TPU:17, one launch (start us, length us, event | category | flops | bytes accessed | tf_op | source)
XLA Modules:
  0.0 31.1 jit_solution(14142749702382463603)
XLA Ops:
  0.0 30.1 %modal_scan.1 = bf16[128,4096]{1,0:T(8,128)(2,1)S(1)} custom-call(bf16[128,12288]{1,0:T(8,128)(2,1)} %proj.1, f32[3,12288]{1,0:T(4,128)} %taps_in.1, f32[16,4096]{1,0:T(8,128)} %bitcast.3, f32[16,4096]{1,0:T(8,128)} %bitcast.4, f32[32,128]{1,0:T(8,128)} %bitcast.5), custom_call_target="tpu_custom_call" | custom-call | tf_op jit(solution)/shard_map/modal_scan/pallas_call | solution.py:459
  30.1 1.0 %copy.7 = bf16[128,4096]{1,0:T(8,128)(2,1)} copy(bf16[128,4096]{1,0:T(8,128)(2,1)S(1)} %modal_scan.1) | data formatting | bytes 2097152

commit v7 on v6

--- a/solution.py
+++ b/solution.py
@@ -55,8 +55,8 @@
     def mate(n):
         return dev(h * n1 + n)
 
-    def ring_order():
-        for dz in (4, 3, 5, 2, 6, 1, 7, 0):
+    def ring_order(order=(4, 3, 5, 2, 6, 1, 7, 0)):
+        for dz in order:
             for hi in range(n1 // RING):
                 if dz or hi:
                     yield lax.rem(e // RING + hi, n1 // RING) * RING + lax.rem(lax.rem(e, RING) + dz, RING)
@@ -251,7 +251,6 @@
 
     tails[1].wait()
     tail_of(0)
-    halo.start()
     par_cps[2].wait()
     par_cps[3].wait()
     for g in range(groups):
@@ -318,6 +317,8 @@
         def _():
             remote(send2, recv2.at[h], s2_sem.at[k], r2_sem.at[h], dev((h + k) * n1 + e)).start()
 
+    halo.start()
+
     power = jnp.ones((modes, LANE), F32)
     for n in range(n1):
         powr[n] = power
@@ -373,7 +374,7 @@
     for n in range(1, n1):
         send3[n] = (pre[n] + powr[n - 1] * after).astype(BF16)
     recv3[mine] = send3[e]
-    for n in list(ring_order())[::-1]:
+    for n in ring_order((0, 1, 7, 2, 6, 4, 3, 5)):
         remote(send3.at[n], recv3.at[mine], s3_sem.at[n], r3_sem.at[mine], mate(n)).start()
     for g in range(split, groups):
         local(g)

time: 31.1 us -> 31.4 us (level)
  no operation moved by 1% of the time
where the time goes in v7:
time: 31.4 us; the launch traced here: 31.3 us
  Pallas kernels  30.3 us (96%)
  local copies, waits for them, and re-layouts  0.97 us (3%)
    pallas_call x1, Pallas kernels, on_device(): pl.pallas_call(functools.partial(kernel, (outer_n, inner_n, rows, channel...  30.3 us
    unnamed x1, local copies, waits for them, and re-layouts  0.97 us

profile of v7, /device:TPU:17, one launch (start us, length us, event | category | flops | bytes accessed | tf_op | source)
XLA Modules:
  0.0 31.3 jit_solution(11686144430647126884)
XLA Ops:
  0.0 30.3 %modal_scan.1 = bf16[128,4096]{1,0:T(8,128)(2,1)S(1)} custom-call(bf16[128,12288]{1,0:T(8,128)(2,1)} %proj.1, f32[3,12288]{1,0:T(4,128)} %taps_in.1, f32[16,4096]{1,0:T(8,128)} %bitcast.3, f32[16,4096]{1,0:T(8,128)} %bitcast.4, f32[32,128]{1,0:T(8,128)} %bitcast.5), custom_call_target="tpu_custom_call" | custom-call | tf_op jit(solution)/shard_map/modal_scan/pallas_call | solution.py:460
  30.3 1.0 %copy.7 = bf16[128,4096]{1,0:T(8,128)(2,1)} copy(bf16[128,4096]{1,0:T(8,128)(2,1)S(1)} %modal_scan.1) | data formatting | bytes 2097152
